TPU v7x, 32 devices: a whole 2x2x4 slice. The times are simulated.
32 devices in a mesh: grp: 2 (over y), ep: 4 (over z), tp: 2 (over x), pp: 2 (over core).
Axes of the slice: x: 2, y: 2, z: 4, core: 2. Of those that a mesh axis runs over, the one named last changes fastest.
Arguments:
- queries: bfloat16 [2048, 8192], P(('grp', 'ep', 'pp'), 'tp'), parts along dimension 0, may hold values from -64 to 64
- suffix_keys: bfloat16 [2048, 512], P(('grp', 'ep', 'pp')), parts along dimension 0, may hold values from -6 to 6
- suffix_values: bfloat16 [2048, 512], P(('grp', 'ep', 'pp')), parts along dimension 0, may hold values from -6 to 6
- prefix_keys: bfloat16 [4096, 512], P(('grp', 'ep', 'pp')), parts along dimension 0, may hold values from -8 to 8
- prefix_values: bfloat16 [4096, 512], P(('grp', 'ep', 'pp')), parts along dimension 0, may hold values from -6 to 6
- prefix_groups: int32 [4096], P(('grp', 'ep', 'pp')), parts along dimension 0, may hold values from 0 to 7, never falling along the last dimension, each value on 1 to 1024 neighbouring positions
- shot_counts: int32 [16], P(('grp', 'ep', 'pp')), parts along dimension 0, may hold values from 1 to 8
- lengths: int32 [16], P(('grp', 'ep', 'pp')), parts along dimension 0, may hold values from 32 to 128
- hidden: bfloat16 [2048, 4096], P(('grp', 'ep', 'pp')), parts along dimension 0, may hold values from -6 to 6
- expert_ids: int32 [2048, 8], P(('grp', 'ep')), parts along dimension 0, may hold values from 0 to 127, all different within a row
- gate_weights: float32 [2048, 8], P(('grp', 'ep')), parts along dimension 0, may hold values from 0.1 to 1
- gate_proj: bfloat16 [4, 4096, 1536], P('ep', 'pp', 'tp'), may hold values from -0.09375 to 0.09375
- up_proj: bfloat16 [4, 4096, 1536], P('ep', 'pp', 'tp'), may hold values from -0.09375 to 0.09375
- down_proj: bfloat16 [4, 1536, 4096], P('ep', 'tp', 'pp'), may hold values from -0.15625 to 0.15625
Outputs:
- context: bfloat16 [2048, 8192], P(('grp', 'ep', 'pp'), 'tp'), parts along dimension 0
- moe_out: bfloat16 [2048, 4096], P(('grp', 'ep'), ('pp', 'tp')), parts along dimension 0
There are 2 independent parts, one for each index of `grp`. A program takes and returns all parts, laid end to end along the dimension named above; an argument that names none is the same for every part. Nothing has to cross between parts.
All inputs are finite; a program needn't handle non-finite values.
Results may differ from a plain program's by a relative error of at most 0.022.
Values may be sent and summed in bfloat16 or wider, within the bound.
No kernel may reach another device: no remote copies, remote signals or barrier semaphores. Data moves between devices by JAX's collectives and lax.ppermute only.
A program may use at most 128 MiB of HBM per device.

v0:
```python
import jax
import jax.numpy as jnp
from jax import lax
from jax.sharding import PartitionSpec as P

D = 4096
HEADS = 64
KVH = 4
HD = 128
TOP = 8
SUFFIX = 128
CAP = 12


NEG = -1e30


def online_update(state_now, scores, visible, value_rows):
    run_max, run_sum, run_acc = state_now
    scores = jnp.where(visible, scores, NEG)
    new_max = jnp.maximum(run_max, jnp.max(scores, axis=-1))
    factor = jnp.exp(run_max - new_max)
    weights = jnp.where(visible, jnp.exp(scores - new_max[..., None]), 0.0)
    new_sum = run_sum * factor + jnp.sum(weights, axis=-1)
    update = jnp.einsum(
        "tkgs,skd->tkgd",
        weights.astype(jnp.bfloat16),
        value_rows,
        preferred_element_type=jnp.float32,
    )
    return (new_max, new_sum, run_acc * factor[..., None] + update)


def shards(
    queries,
    suffix_keys,
    suffix_values,
    prefix_keys,
    prefix_values,
    prefix_groups,
    shot_counts,
    lengths,
    hidden,
    expert_ids,
    gate_weights,
    gate_proj,
    up_proj,
    down_proj,
):
    tok_rows = queries.shape[0]
    local_heads = queries.shape[1] // HD
    head_group = HEADS // KVH
    kv_heads = max(1, local_heads // head_group)
    per_kv = min(local_heads, head_group)
    kv_width = kv_heads * HD
    kv_first = lax.axis_index("tp") * local_heads // head_group
    score_scale = HD ** (-0.5)

    def select_heads(block):
        return lax.dynamic_slice_in_dim(block, kv_first * HD, kv_width, 1)

    query_heads = queries.reshape(tok_rows, kv_heads, per_kv, HD)
    question_count = shot_counts.shape[0]
    tok_shots = jnp.broadcast_to(shot_counts[:, None], (question_count, SUFFIX)).reshape(-1)
    tok_length = jnp.broadcast_to(lengths[:, None], (question_count, SUFFIX)).reshape(-1)

    def score_of(key_rows):
        shaped = key_rows.reshape(key_rows.shape[0], kv_heads, HD)
        return (
            jnp.einsum("tkgd,skd->tkgs", query_heads, shaped, preferred_element_type=jnp.float32)
            * score_scale
        )

    initial = (
        jnp.full((tok_rows, kv_heads, per_kv), NEG, jnp.float32),
        jnp.zeros((tok_rows, kv_heads, per_kv), jnp.float32),
        jnp.zeros((tok_rows, kv_heads, per_kv, HD), jnp.float32),
    )
    key_rows = lax.all_gather(select_heads(prefix_keys), ("ep", "pp"), axis=0, tiled=True)
    value_rows = lax.all_gather(select_heads(prefix_values), ("ep", "pp"), axis=0, tiled=True)
    segment_ids = lax.all_gather(prefix_groups, ("ep", "pp"), axis=0, tiled=True)
    visible = (segment_ids[None, :] < tok_shots[:, None])[:, None, None, :]
    state_now = online_update(
        initial, score_of(key_rows), visible, value_rows.reshape(value_rows.shape[0], kv_heads, HD)
    )
    question_of = jnp.arange(tok_rows, dtype=jnp.int32) // SUFFIX
    position = jnp.arange(tok_rows, dtype=jnp.int32) % SUFFIX
    own_seen = (
        (question_of[:, None] == question_of[None, :])
        & (position[None, :] <= position[:, None])
        & (position[None, :] < tok_length[None, :])
    )
    own_values = select_heads(suffix_values)
    run_max, run_sum, run_acc = online_update(
        state_now,
        score_of(select_heads(suffix_keys)),
        own_seen[:, None, None, :],
        own_values.reshape(tok_rows, kv_heads, HD),
    )
    attended = run_acc / run_sum[..., None]
    attended = jnp.where((position < tok_length)[:, None, None, None], attended, 0.0)
    context = attended.reshape(tok_rows, local_heads * HD).astype(jnp.bfloat16)
    ep_size = lax.axis_size("ep")
    pp_size = lax.axis_size("pp")
    tp_size = lax.axis_size("tp")
    pp_index = lax.axis_index("pp")
    routed = expert_ids.reshape(pp_size, tok_rows, TOP)
    gate_share = gate_weights.reshape(pp_size, tok_rows, TOP)
    matches = routed[..., None] == jnp.arange(ep_size, dtype=jnp.int32)
    taken = jnp.sum(matches.astype(jnp.int32), axis=2)
    shares = jnp.sum(jnp.where(matches, gate_share[..., None], 0.0), axis=2)
    slot_index = jnp.cumsum(taken, axis=1) - taken
    served = (taken > 0) & (slot_index < CAP)
    slot_table = served[..., None] & (slot_index[..., None] == jnp.arange(CAP, dtype=jnp.int32))
    own_slots = lax.dynamic_index_in_dim(slot_table, pp_index, 0, keepdims=False)
    rows_in = hidden.reshape(tok_rows, pp_size, D // pp_size)
    outgoing = jnp.einsum(
        "tec,tpd->epcd", own_slots.astype(jnp.bfloat16), rows_in, preferred_element_type=jnp.float32
    ).astype(jnp.bfloat16)
    w_gate = gate_proj[0]
    w_up = up_proj[0]
    w_down = down_proj[0]
    unit_width = w_gate.shape[1]
    half_width = w_gate.shape[0]
    row_block = lax.all_to_all(
        outgoing.reshape(ep_size * pp_size, CAP, half_width),
        ("ep", "pp"),
        split_axis=0,
        concat_axis=0,
        tiled=True,
    )
    gate_part = jnp.einsum("sxd,df->sxf", row_block, w_gate, preferred_element_type=jnp.float32)
    up_part = jnp.einsum("sxd,df->sxf", row_block, w_up, preferred_element_type=jnp.float32)
    gate_full, up_full = (
        lax.psum(gate_part.astype(jnp.bfloat16), "pp").astype(jnp.float32),
        lax.psum(up_part.astype(jnp.bfloat16), "pp").astype(jnp.float32),
    )
    active = (
        (jax.nn.silu(gate_full) * up_full)
        .astype(jnp.bfloat16)
        .reshape(ep_size * pp_size * CAP, unit_width)
    )
    col_width = w_down.shape[1] // tp_size
    result = lax.psum_scatter(
        lax.dot_general(
            w_down, active, (((0,), (1,)), ((), ())), preferred_element_type=jnp.float32
        ).astype(jnp.bfloat16),
        "tp",
        scatter_dimension=0,
        tiled=True,
    )
    expert_out = result.reshape(col_width, ep_size, pp_size, CAP)
    returned = lax.all_to_all(expert_out, "ep", split_axis=1, concat_axis=1, tiled=True)
    weight_table = jnp.where(slot_table, shares[..., None], 0.0)
    combined = jnp.einsum("ptec,xepc->ptx", weight_table, returned.astype(jnp.float32))
    moe_out = combined.reshape(pp_size * tok_rows, col_width).astype(jnp.bfloat16)
    return (context, moe_out)


def solution(mesh):
    placed = (
        P(("grp", "ep", "pp"), "tp"),
        P(("grp", "ep", "pp"), None),
        P(("grp", "ep", "pp"), None),
        P(("grp", "ep", "pp"), None),
        P(("grp", "ep", "pp"), None),
        P(("grp", "ep", "pp")),
        P(("grp", "ep", "pp")),
        P(("grp", "ep", "pp")),
        P(("grp", "ep", "pp"), None),
        P(("grp", "ep"), None),
        P(("grp", "ep"), None),
        P("ep", "pp", "tp"),
        P("ep", "pp", "tp"),
        P("ep", "tp", "pp"),
    )
    return jax.shard_map(
        shards,
        mesh=mesh,
        in_specs=placed,
        out_specs=(P(("grp", "ep", "pp"), "tp"), P(("grp", "ep"), ("pp", "tp"))),
        check_vma=False,
    )
```

profile of v0, /device:TPU:0, one launch (start us, length us, event | category | flops | bytes accessed | tf_op | source)
XLA Modules:
  0.0 152.0 jit_solution(6718076928422719528)
XLA Ops:
  8.1 0.9 convert_reduce_fusion
  9.4 1.5 convolution_convert_fusion
  10.9 21.7 %all_to_all.10 = bf16[8,12,2048]{2,1,0:T(8,128)(2,1)S(1)} all-to-all(bf16[8,12,2048]{2,1,0:T(8,128)(2,1)S(1)} %bitcast.124), channel_id=1, replica_groups=mesh['grp'=2,'ep'=4,'tp'=2,'pp'=2] {'ep','pp'}, dimensions={0} | all-to-all | bytes 786432 | tf_op jit(solution)/shard_map/all_to_all | solution.py:125
  32.7 3.1 %fusion.30 = bf16[8,12,768]{2,1,0:T(8,128)(2,1)} fusion(bf16[8,12,2048]{2,1,0:T(8,128)(2,1)S(1)} %all_to_all.10, bf16[1,2048,768]{2,1,0:T(8,128)(2,1)} %param.25), kind=kOutput, calls=%fused_computation.32 | convolution fusion | flops 302063616 | bytes 3686400 | tf_op jit(solution)/shard_map/sxd,df->sxf/dot_general | solution.py:132
  35.8 1.3 fusion.33
  37.2 17.5 %all-reduce.3.cloned.1.call-done = (bf16[8,12,768]{2,1,0:T(8,128)(2,1)}, bf16[8,12,768]{2,1,0:T(8,128)(2,1)}) async-done(((bf16[8,12,768]{2,1,0:T(8,128)(2,1)}, bf16[8,12,768]{2,1,0:T(8,128)(2,1)}), (bf16[8,12,768]{2,1,0:T(8,128)(2,1)}, bf16[8,12,768]{2,1,0:T(8,128)(2,1)})) %all-reduce.3.cloned.1.call-update) | async-done | bytes 294928 | tf_op jit(solution)/shard_map/psum | solution.py:136
  54.7 1.1 fusion.52
  55.9 1.4 fusion.17
  57.4 0.9 constant_dynamic-slice_fusion.3
  59.2 1.6 %constant_dynamic-slice_fusion.2 = bf16[256,256]{1,0:T(8,128)(2,1)} fusion(bf16[256,512]{1,0:T(8,128)(2,1)} %param.18, s32[]{:T(128)S(6)} %select_n.82), kind=kLoop, calls=%fused_computation.76 | loop fusion | bytes 262148 | tf_op jit(solution)/shard_map/dynamic_slice | solution.py:60
  60.8 12.1 %all-gather = s32[8,1,256]{2,1,0:T(1,128)S(1)} all-gather(s32[1,1,256]{2,1,0:T(1,128)S(1)} %bitcast.136), channel_id=1, replica_groups=mesh['grp'=2,'ep'=4,'tp'=2,'pp'=2] {'ep','pp'}, dimensions={0}, use_global_device_ids=true | all-gather | bytes 9216 | tf_op jit(solution)/shard_map/all_gather | solution.py:81
  73.6 2.4 %copy.115 = bf16[16,8,32,128]{3,2,1,0:T(8,128)(2,1)} copy(bf16[16,8,32,128]{3,1,2,0:T(8,128)(2,1)} %bitcast.127) | data formatting | bytes 2097152
  76.1 0.8 constant_dynamic-slice_fusion
  78.3 3.2 %fusion.24 = (f32[128,2,16]{0,2,1:T(8,128)S(1)}, f32[2,128,128,16]{2,1,3,0:T(8,128)}) fusion(pred[128,128]{0,1:T(8,128)(4,1)S(1)} %and_and_fusion, bf16[128,2,128,1]{0,2,3,1:T(8,128)(2,1)S(1)} %bitcast.132, bf16[128,2,16,128]{3,2,1,0:T(8,128)(2,1)} %bitcast.122), kind=kOutput, calls=%fused_computation.27 | convolution fusion | flops 135786496 | bytes 3244032 | tf_op jit(solution)/shard_map/tkgd,skd->tkgs/dot_general | solution.py:70
  81.5 1.0 reshape.224
  82.4 0.9 copy.97
  83.3 3.5 %all-to-all-start.1 = ((bf16[1024,4,2,12]{0,2,3,1:T(2,128)(2,1)}), bf16[1024,4,2,12]{0,2,3,1:T(2,128)(2,1)S(1)}, u32[]{:S(2)}, u32[]{:S(2)}) async-start(bf16[1024,4,2,12]{0,2,3,1:T(2,128)(2,1)} %copy.97), calls=%async_computation.2 | async-start | bytes 393216 | tf_op jit(solution)/shard_map/all_to_all | solution.py:153
  86.9 16.2 %bitcast_reduce_fusion = (f32[128,2,16]{0,2,1:T(8,128)S(1)}, f32[2,2048,128,16]{2,1,3,0:T(8,128)}) fusion(pred[2048]{0:T(1024)(128)(4,1)S(1)} %reshape.228, bf16[2048,2,128,1]{0,2,3,1:T(8,128)(2,1)} %bitcast.125, bf16[128,2,16,128]{3,2,1,0:T(8,128)(2,1)} %bitcast.123), kind=kOutput, calls=%fused_computation.1 | convolution fusion | flops 2172645376 | bytes 35670016 | tf_op jit(solution)/shard_map/tkgd,skd->tkgs/dot_general | solution.py:70
  103.1 15.5 %fusion.2 = f32[128,2,16]{0,2,1:T(8,128)S(1)} fusion(f32[2,2048,128,16]{2,1,3,0:T(8,128)} %get-tuple-element.22, f32[128,2,16]{0,2,1:T(8,128)S(1)} %get-tuple-element.20, pred[2048]{0:T(1024)(128)(4,1)S(1)} %reshape.228), kind=kLoop, calls=%fused_computation.5 | loop fusion | flops 41938944 | bytes 33589248 | tf_op jit(solution)/shard_map/reduce_sum | solution.py:24
  119.8 2.0 %fusion.36 = f32[2,128,128,16]{2,1,3,0:T(8,128)} fusion(bf16[128,2,128,1]{0,2,3,1:T(8,128)(2,1)S(1)} %bitcast.131, f32[2,128,128,16]{2,1,3,0:T(8,128)S(1)} %copy-done.1, f32[128,2,16]{0,2,1:T(8,128)S(1)} %get-tuple-element.19, pred[128,128]{0,1:T(8,128)(4,1)S(1)} %and_and_fusion), kind=kOutput, calls=%fused_computation.34 | convolution fusion | flops 136839168 | bytes 4292608 | tf_op jit(solution)/shard_map/tkgs,skd->tkgd/dot_general | solution.py:25
  121.8 2.3 %copy.87 = bf16[2048,256]{0,1:T(8,128)(2,1)} copy(bf16[2048,256]{1,0:T(8,128)(2,1)} %all-gather.6.cloned.1.call-done) | data formatting | bytes 2097152 | tf_op jit(solution)/shard_map/all_gather | solution.py:80
  124.1 17.1 %fusion.22 = bf16[128,2,16,128]{0,3,2,1:T(8,128)(2,1)} fusion(f32[2,128,128,16]{2,1,3,0:T(8,128)} %fusion.36, bf16[2048,2,128,1]{0,2,3,1:T(8,128)(2,1)} %bitcast.128, f32[2,2048,128,16]{2,1,3,0:T(8,128)} %get-tuple-element.22, f32[128,2,16]{0,2,1:T(8,128)S(1)} %get-tuple-element.20, pred[2048]{0:T(1024)(128)(4,1)S(1)} %reshape.228, ...), kind=kOutput, calls=%fused_computation.22 | convolution fusion | flops 2192572416 | bytes 37816448 | tf_op jit(solution)/shard_map/tkgs,skd->tkgd/dot_general | solution.py:25
  141.1 2.3 %copy.99 = bf16[128,4096]{1,0:T(8,128)(2,1)} copy(bf16[128,4096]{0,1:T(8,128)(2,1)} %bitcast.129) | data formatting | bytes 2097152
  143.4 1.1 fusion.29
  (50 shorter events, 3.4 us)
Async XLA Ops:
  8.0 47.9 %copy-start = (bf16[1,768,2048]{2,1,0:T(8,128)(2,1)S(1)}, bf16[1,768,2048]{2,1,0:T(8,128)(2,1)}, u32[]{:S(2)}) copy-start(bf16[1,768,2048]{2,1,0:T(8,128)(2,1)} %param.27) | copy-start | bytes 9437188
  8.0 46.7 %all-reduce.3.cloned.1.call-start = ((), (), s32[]{:S(2)}) async-start(), calls=%async_computation.6 | async-start | bytes 786432 | tf_op jit(solution)/shard_map/psum | solution.py:136
  10.9 24.9 %copy-start.2 = (bf16[1,2048,768]{2,1,0:T(8,128)(2,1)S(1)}, bf16[1,2048,768]{2,1,0:T(8,128)(2,1)}, u32[]{:S(2)}) copy-start(bf16[1,2048,768]{2,1,0:T(8,128)(2,1)} %param.26) | copy-start | bytes 9437188
  37.1 23.7 %copy-start.7 = (s32[256]{0:T(256)S(1)}, s32[256]{0:T(256)}, u32[]{:S(2)}) copy-start(s32[256]{0:T(256)} %param.19) | copy-start | bytes 3076
  37.1 44.3 %reduce-scatter.2.cloned.1.call-start = ((), (), s32[]{:S(2)}) async-start(), calls=%async_computation.5 | async-start | bytes 589824 | tf_op jit(solution)/shard_map/reduce_scatter | solution.py:144
  55.9 22.0 %copy-start.3 = (s32[256,8]{0,1:T(8,128)S(1)}, s32[256,8]{0,1:T(8,128)}, u32[]{:S(2)}) copy-start(s32[256,8]{0,1:T(8,128)} %param.23) | copy-start | bytes 24580
  55.9 21.9 %copy-start.6 = (f32[256,8]{0,1:T(8,128)S(1)}, f32[256,8]{0,1:T(8,128)}, u32[]{:S(2)}) copy-start(f32[256,8]{0,1:T(8,128)} %param.24) | copy-start | bytes 24580
  57.3 18.8 %copy-start.4 = (bf16[128,512]{1,0:T(8,128)(2,1)S(1)}, bf16[128,512]{1,0:T(8,128)(2,1)}, u32[]{:S(2)}) copy-start(bf16[128,512]{1,0:T(8,128)(2,1)} %param.16) | copy-start | bytes 393220
  57.3 29.6 %all-gather.4.cloned.1.call-start = ((), (), s32[]{:S(2)}) async-start(), calls=%async_computation.3 | async-start | bytes 1179648 | tf_op jit(solution)/shard_map/all_gather | solution.py:79
  59.1 62.7 %all-gather.6.cloned.1.call-start = ((), (), s32[]{:S(2)}) async-start(), calls=%async_computation.4 | async-start | bytes 1179648 | tf_op jit(solution)/shard_map/all_gather | solution.py:80
  77.7 0.6 copy-start.8
  83.3 60.1 %all-to-all-start.1 = ((bf16[1024,4,2,12]{0,2,3,1:T(2,128)(2,1)}), bf16[1024,4,2,12]{0,2,3,1:T(2,128)(2,1)S(1)}, u32[]{:S(2)}, u32[]{:S(2)}) async-start(bf16[1024,4,2,12]{0,2,3,1:T(2,128)(2,1)} %copy.97), calls=%async_computation.2 | async-start | bytes 393216 | tf_op jit(solution)/shard_map/all_to_all | solution.py:153
  103.1 15.5 %copy-start.1 = (f32[2,128,128,16]{2,1,3,0:T(8,128)S(1)}, f32[2,128,128,16]{2,1,3,0:T(8,128)}, u32[]{:S(2)}) copy-start(f32[2,128,128,16]{2,1,3,0:T(8,128)} %get-tuple-element.24) | copy-start | bytes 6291460
  119.8 4.3 %copy-start.5 = (f32[128,2,16]{0,2,1:T(8,128)S(1)}, f32[128,2,16]{0,2,1:T(8,128)}, u32[]{:S(2)}) copy-start(f32[128,2,16]{0,2,1:T(8,128)} %get-tuple-element.17) | copy-start | bytes 49156
  119.8 4.3 %copy-start.9 = (pred[128]{0:T(512)(128)(4,1)S(1)}, pred[128]{0:T(512)(128)(4,1)}, u32[]{:S(2)}) copy-start(pred[128]{0:T(512)(128)(4,1)} %copy-done.8) | copy-start | bytes 388
Sparse Core Ops, SparseCore 0:
  37.2 17.4 all-reduce.2
  57.5 14.3 reduce-scatter.1
Sparse Core Ops, SparseCore 1:
  59.4 25.0 all-gather.3
  86.0 20.6 all-gather.5
where the time goes:
time: 153 us; the launch traced here: 152 us
  matrix products  46.9 us (31%)
  blocking collectives  33.9 us (22%)
  other arithmetic  19.1 us (12%)
  waiting for transfers between devices  17.6 us (12%)
  between operations  17 us (11%)
  local copies, waits for them, and re-layouts  13.7 us (9%)
  starting transfers between devices  3.71 us (2%)
    all_to_all x1, blocking collectives, shards(): lax.all_to_all(outgoing.reshape(ep_size * pp_size, CAP, half_width), ('ep...  21.7 us
    dot_general x2, matrix products, score_of(): jnp.einsum('tkgd,skd->tkgs', query_heads, shaped, preferred_element_type=...  19.3 us
    dot_general x2, matrix products, online_update(): jnp.einsum('tkgs,skd->tkgd', weights.astype(jnp.bfloat16), value_rows, pr...  19.1 us
    psum x1, waiting for transfers between devices, shards(): lax.psum(up_part.astype(jnp.bfloat16), 'pp').astype(jnp.float32)  17.5 us
    reduce_sum x2, other arithmetic, online_update(): new_sum = run_sum * factor + jnp.sum(weights, axis=-1)  16.1 us
    all_gather x1, blocking collectives, shards(): lax.all_gather(prefix_groups, ('ep', 'pp'), axis=0, tiled=True)  12.1 us
    unnamed x24, local copies, waits for them, and re-layouts  5.91 us
    all_to_all x1, starting transfers between devices, shards(): lax.all_to_all(expert_out, 'ep', split_axis=1, concat_axis=1, tiled=True)  3.55 us
  transfers between devices with their start and end apart: 5, of which 1 were waited for; matrix products, arithmetic and copies ran while one was open for 45% of the time, Pallas kernels for 0%

commit v1 on v0

v1 whole, which is shorter than its diff:
```python
import functools
import math

import jax
import jax.numpy as jnp
from jax import lax
from jax.experimental import pallas as pl
from jax.experimental.pallas import tpu as pltpu
from jax.sharding import PartitionSpec as P


HEADS = 64
KVH = 4
HD = 128
TOP = 8
CAP = 12

NEG = -1e30
SCORE_SCALE = HD ** (-0.5) * math.log2(math.e)
GROUP_ROWS = 16
STACK = 2
ATT_MIB = 24
VMEM_ALL = 67043328
SELECT_KIB = 960


BF = jnp.bfloat16
F32 = jnp.float32
VMEM = pl.BlockSpec(memory_space=pltpu.VMEM)
ANY = pl.BlockSpec(memory_space=pl.ANY)
HBM = pl.BlockSpec(memory_space=pltpu.HBM)


def dot(a, b, dims=(((1,), (0,)), ((), ()))):
    return lax.dot_general(a, b, dims, preferred_element_type=F32)


def params(mib=40, **kw):
    return pltpu.CompilerParams(vmem_limit_bytes=mib << 20, **kw)


def cost(flops, nbytes):
    return pl.CostEstimate(flops=int(flops), bytes_accessed=int(nbytes), transcendentals=0)


def attend_kernel(cfg, facts_ref, *refs):
    per_kv, width, head_block, rows_of, first, previous, last, waits = cfg
    refs = list(refs)
    q_ref = refs.pop(0)
    if first:
        sk_ref, sv_ref = refs.pop(0), refs.pop(0)
    packs = [refs.pop(0) for _ in rows_of]
    before = [(refs.pop(0), refs.pop(0)) for _ in range(previous)]
    del refs[:waits]
    tok, columns = q_ref.shape
    local_heads = columns // HD
    stack = min(STACK, per_kv)
    shots = facts_ref[0:1, 0:1]
    length = jnp.broadcast_to(facts_ref[8:9, :], (tok, 128))
    lane = lax.broadcasted_iota(jnp.int32, (tok, 128), 1)
    live = lax.broadcasted_iota(jnp.int32, (tok, HD), 0).astype(F32) < length
    if last:
        (ctx_ref,) = refs
    else:
        ctx_ref, lse_ref = refs
        lse_ref[...] = jnp.zeros((tok, 128), F32)
    for kv in range(local_heads // per_kv):
        col = slice(kv * HD, (kv + 1) * HD)
        blocks = []
        if first:
            start = pl.multiple_of(head_block(lax.axis_index("tp")) * width + kv * HD, HD)
            across = lax.broadcasted_iota(jnp.int32, (tok, tok), 1)
            line = lax.broadcasted_iota(jnp.int32, (tok, tok), 0)
            seen = (across <= line) & (across.astype(F32) < length)
            bias = jnp.where(seen, 0.0, NEG).astype(F32)
            bias = jnp.concatenate([bias] * stack, axis=0)
            blocks.append((sk_ref[:, pl.ds(start, HD)], sv_ref[:, pl.ds(start, HD)], bias))
        for rows, ref in zip(rows_of, packs):
            lines = max(1, rows // width)
            groups = [ref[2 * rows + n : 2 * rows + n + 1, : rows // lines] for n in range(lines)]
            groups = groups[0] if lines == 1 else jnp.concatenate(groups, axis=1)
            groups = groups.astype(F32)
            bias = jnp.where(groups < jnp.broadcast_to(shots, groups.shape), 0.0, NEG).astype(F32)
            blocks.append((ref[0:rows, col], ref[rows : 2 * rows, col], bias))
        blocks = [(k, jnp.concatenate([v, jnp.ones_like(v)], axis=1), b) for k, v, b in blocks]

        def group(base):
            ats = [slice((base + i) * HD, (base + i + 1) * HD) for i in range(stack)]
            q = jnp.concatenate([q_ref[:, at] for at in ats], axis=0)
            scores = [
                dot(q, k, (((1,), (1,)), ((), ()))) * SCORE_SCALE + bias for k, _, bias in blocks
            ]
            peak = None
            for s in scores:
                for j in range(0, s.shape[1], 128):
                    part = s[:, j : j + 128]
                    peak = part if peak is None else jnp.maximum(peak, part)
            peak = jnp.max(peak, axis=1, keepdims=True)
            update = None
            for s, (_, v, _) in zip(scores, blocks):
                term = dot(jnp.exp2(s - peak).astype(BF), v)
                update = term if update is None else update + term
            for i, at in enumerate(ats):
                r = slice(i * tok, (i + 1) * tok)
                top, total = update[r, :HD], update[r, HD:]
                mine = jnp.broadcast_to(peak[r], (tok, HD))
                if not last:
                    ctx_ref[:, at] = (top / total).astype(BF)
                    level = mine + jnp.log2(total)
                    lse_ref[...] = jnp.where(lane == base + i, level, lse_ref[...])
                    continue
                bound, levels = mine, []
                for _, lse in before:
                    level = jnp.broadcast_to(lse[:, base + i : base + i + 1], (tok, HD))
                    levels.append(level)
                    bound = jnp.maximum(bound, level)
                if before:
                    factor = jnp.exp2(mine - bound)
                    top, total = top * factor, total * factor
                for (ctx, _), level in zip(before, levels):
                    factor = jnp.exp2(level - bound)
                    top = top + ctx[:, at].astype(F32) * factor
                    total = total + factor
                ctx_ref[:, at] = jnp.where(live, top / total, 0.0).astype(BF)

        for i in range(0, per_kv, stack):
            group(kv * per_kv + i)


def attend(queries, facts, own, packs, before, last, per_kv, width, head_block, waits=()):
    tok, columns = queries.shape
    local_heads = columns // HD
    first = own is not None
    rows_of = tuple((p.shape[0] - GROUP_ROWS) // 2 for p in packs)
    cfg = (per_kv, width, head_block, rows_of, first, len(before), last, len(waits))
    operands = [facts, queries] + (list(own) if first else []) + list(packs)
    for pair in before:
        operands += list(pair)
    context = jax.ShapeDtypeStruct((tok, columns), BF)
    level = jax.ShapeDtypeStruct((tok, 128), F32)
    keys = sum(rows_of) + (tok if first else 0)
    return pl.pallas_call(
        functools.partial(attend_kernel, cfg),
        out_shape=context if last else [context, level],
        in_specs=[VMEM] * len(operands) + [ANY] * len(waits),
        out_specs=VMEM if last else [VMEM, VMEM],
        compiler_params=params(ATT_MIB),
        cost_estimate=cost(8 * tok * local_heads * keys * HD, 4 * tok * columns),
        name="attend",
    )(*operands, *waits)


def earlier(tok):
    line = lax.broadcasted_iota(jnp.int32, (tok, tok), 0)
    lane = lax.broadcasted_iota(jnp.int32, (tok, tok), 1)
    return jnp.where(line < lane, 1.0, 0.0).astype(BF)


def routes(ids, expert_of, weights=None):
    shape = expert_of.shape
    taken = jnp.zeros(shape, F32)
    share = jnp.zeros(shape, F32)
    for k in range(TOP):
        match = jnp.broadcast_to(ids[k : k + 1, :], shape) == expert_of
        taken = jnp.where(match, 1.0, taken)
        if weights is not None:
            share = share + jnp.where(match, jnp.broadcast_to(weights[k : k + 1, :], shape), 0.0)
    slot = dot(taken.astype(BF), earlier(shape[1])).astype(jnp.int32)
    return taken, slot, share


def pack_kernel(width, head_block, k_ref, v_ref, g_ref, shots_ref, len_ref, out_ref, facts_ref, *scratch):
    groups_ref, held_ref, line_ref, one_ref, two_ref, sem = scratch
    rows = k_ref.shape[0]
    first = pl.multiple_of(head_block(lax.axis_index("tp")) * width, 128)
    copies = [pltpu.make_async_copy(g_ref, groups_ref, sem.at[2])]
    for n, ref in enumerate((k_ref, v_ref)):
        place = held_ref.at[n * rows : (n + 1) * rows, :]
        copies.append(pltpu.make_async_copy(ref.at[:, pl.ds(first, width)], place, sem.at[n]))
    copies.append(pltpu.make_async_copy(shots_ref, one_ref, sem.at[4]))
    copies.append(pltpu.make_async_copy(len_ref, two_ref, sem.at[5]))
    for copy in copies:
        copy.start()
    copies[3].wait()
    copies[4].wait()
    line_ref[0:8, :] = jnp.full((8, 128), one_ref[0].astype(F32))
    line_ref[8:16, :] = jnp.full((8, 128), two_ref[0].astype(F32))
    facts = pltpu.make_async_copy(line_ref, facts_ref, sem.at[4])
    facts.start()
    copies[0].wait()
    groups = groups_ref[...].astype(F32)
    pad = jnp.full((GROUP_ROWS - groups.shape[0], groups.shape[1]), 0.0, F32)
    groups = jnp.concatenate([groups, pad], axis=0)
    if groups.shape[1] < width:
        filler = jnp.zeros((GROUP_ROWS, width - groups.shape[1]), F32)
        groups = jnp.concatenate([groups, filler], axis=1)
    held_ref[2 * rows :, :] = groups.astype(BF)
    copies[1].wait()
    copies[2].wait()
    store = pltpu.make_async_copy(held_ref, out_ref, sem.at[3])
    store.start()
    facts.wait()
    store.wait()


def make_pack(keys, values, groups, shots, lengths, width, head_block):
    rows = keys.shape[0]
    lines = max(1, rows // width)
    shape = (2 * rows + GROUP_ROWS, width)
    return pl.pallas_call(
        functools.partial(pack_kernel, width, head_block),
        out_shape=[jax.ShapeDtypeStruct(shape, BF), jax.ShapeDtypeStruct((16, 128), F32)],
        in_specs=[HBM] * 5,
        out_specs=[HBM] * 2,
        scratch_shapes=[
            pltpu.VMEM((lines, rows // lines), jnp.int32),
            pltpu.VMEM(shape, BF),
            pltpu.VMEM((16, 128), F32),
            pltpu.SMEM((1,), jnp.int32),
            pltpu.SMEM((1,), jnp.int32),
            pltpu.SemaphoreType.DMA((6,)),
        ],
        compiler_params=pltpu.CompilerParams(vmem_limit_bytes=VMEM_ALL),
        cost_estimate=cost(0, 4 * rows * width * 4),
        name="pack",
    )(keys, values, groups.reshape(lines, rows // lines), shots, lengths)


def target(me, n, size):
    return me ^ n if size & (size - 1) == 0 else lax.rem(me + n, size)


def select_kernel(cfg, place_ref, ids_ref, *refs):
    experts, parts = cfg
    hidden, outs = refs[:parts], refs[parts : parts + experts]
    own_ref, held_ref, here_ref, sem = refs[parts + experts :]
    tok, model = hidden[0].shape
    half = model // parts
    me = lax.axis_index("pp")
    column = pl.multiple_of(me * half, 128)
    copies = [pltpu.make_async_copy(ids_ref, own_ref, sem.at[0])]
    copies.append(pltpu.make_async_copy(place_ref, here_ref, sem.at[1 + parts]))
    for n in range(parts):
        source = hidden[n].at[:, pl.ds(column, half)]
        rows = held_ref.at[n * tok : (n + 1) * tok, :]
        copies.append(pltpu.make_async_copy(source, rows, sem.at[1 + n]))
    for copy in copies:
        copy.start()
    copies[0].wait()
    copies[1].wait()
    per = parts * CAP
    lines = experts * per
    row = lax.broadcasted_iota(jnp.int32, (lines, tok), 0)
    expert = target(here_ref[0], row // per, experts)
    picks = []
    for n in range(parts):
        block = lax.rem(me + parts - n, parts)
        ids = own_ref[:, pl.ds(pl.multiple_of(block * tok, tok), tok)]
        taken, slot, _ = routes(ids, expert)
        place = row % per
        chosen = (taken > 0.0) & (slot == place % CAP) & (place // CAP == block)
        picks.append(jnp.where(chosen, 1.0, 0.0))
    pick = jnp.concatenate(picks, axis=1)
    for copy in copies[2:]:
        copy.wait()
    for e in range(experts):
        outs[e][...] = dot(pick[e * per : (e + 1) * per, :].astype(BF), held_ref[...]).astype(BF)


def select(place, ids, hidden, experts, parts):
    tok, model = hidden[0].shape
    half = model // parts
    return pl.pallas_call(
        functools.partial(select_kernel, (experts, parts)),
        out_shape=[jax.ShapeDtypeStruct((parts * CAP, half), BF)] * experts,
        in_specs=[HBM] * (2 + parts),
        out_specs=[VMEM] * experts,
        scratch_shapes=[
            pltpu.VMEM(ids.shape, jnp.int32),
            pltpu.VMEM((parts * tok, half), BF),
            pltpu.SMEM((1,), jnp.int32),
            pltpu.SemaphoreType.DMA((2 + parts,)),
        ],
        compiler_params=pltpu.CompilerParams(vmem_limit_bytes=VMEM_ALL - (SELECT_KIB << 10)),
        cost_estimate=cost(4 * tok * model * experts * CAP, 2 * tok * model),
        name="select",
    )(place, ids, *hidden)


def mark_kernel(wait_ref, out_ref):
    out_ref[...] = jnp.zeros_like(out_ref)


def mark(wait, flops):
    return pl.pallas_call(
        mark_kernel,
        out_shape=jax.ShapeDtypeStruct((8, 128), F32),
        in_specs=[ANY],
        out_specs=VMEM,
        compiler_params=params(1),
        cost_estimate=cost(flops, 4096),
        name="mark",
    )(wait)


def gateup_kernel(pieces, waits, gate_ref, up_ref, *refs):
    out_ref = refs[pieces + waits]
    units = gate_ref.shape[2]
    x = jnp.concatenate([r[...].astype(F32) for r in refs[:pieces]], axis=0).astype(BF)
    for n, w_ref in enumerate((gate_ref, up_ref)):
        out_ref[:, n * units : (n + 1) * units] = dot(x, w_ref[0]).astype(BF)


def gateup(pieces, gate_proj, up_proj, waits=()):
    _, model, units = gate_proj.shape
    rows = sum(p.shape[0] for p in pieces)
    return pl.pallas_call(
        functools.partial(gateup_kernel, len(pieces), len(waits)),
        out_shape=jax.ShapeDtypeStruct((rows, 2 * units), BF),
        in_specs=[VMEM] * (2 + len(pieces)) + [ANY] * len(waits),
        out_specs=VMEM,
        compiler_params=params(16),
        cost_estimate=cost(4 * rows * model * units, 4 * model * units),
        name="gateup",
    )(gate_proj, up_proj, *pieces, *waits)


def down_kernel(splits, waits, mine_ref, other_ref, down_ref, *outs):
    outs = outs[waits:]
    units = mine_ref.shape[1] // 2
    total = mine_ref[...].astype(F32)
    for n in range(other_ref.shape[0]):
        total = total + other_ref[n].astype(F32)
    gate, up = total[:, :units], total[:, units:]
    active = (gate / (1.0 + jnp.exp(-gate)) * up).astype(BF)
    width = down_ref.shape[2] // splits
    me = lax.axis_index("tp")
    for n in range(splits):
        at = pl.ds(pl.multiple_of(target(me, n, splits) * width, 128), width)
        outs[n][...] = dot(active, down_ref[0, :, at]).astype(outs[n].dtype)


def down(mine, other, down_proj, splits, waits=()):
    rows = mine.shape[0]
    _, units, model = down_proj.shape
    shapes = [jax.ShapeDtypeStruct((rows, model // splits), F32 if n == 0 else BF) for n in range(splits)]
    return pl.pallas_call(
        functools.partial(down_kernel, splits, len(waits)),
        out_shape=shapes,
        in_specs=[VMEM] * 3 + [ANY] * len(waits),
        out_specs=[VMEM] * splits,
        compiler_params=params(16),
        cost_estimate=cost(2 * rows * model * units, 2 * model * units),
        name="down",
    )(mine, other, down_proj, *waits)


def join_kernel(experts, count, waits, *refs):
    parts, outs = refs[:count], refs[count + waits :]
    per = parts[0].shape[0] // experts
    for n in range(experts):
        at = slice(n * per, (n + 1) * per)
        total = parts[0][at, :]
        for p in parts[1:]:
            total = total + p[at, :].astype(F32)
        outs[n][...] = total.astype(BF)


def join(parts, experts, waits=()):
    rows, width = parts[0].shape
    return pl.pallas_call(
        functools.partial(join_kernel, experts, len(parts), len(waits)),
        out_shape=[jax.ShapeDtypeStruct((rows // experts, width), BF)] * experts,
        in_specs=[VMEM] * len(parts) + [ANY] * len(waits),
        out_specs=[VMEM] * experts,
        compiler_params=params(8),
        cost_estimate=cost(rows * width, 8 * rows * width),
        name="join",
    )(*parts, *waits)


def table_kernel(experts, parts, waits, place_ref, ids_ref, weight_ref, *refs):
    high_ref, low_ref, here_ref, sem = refs[waits:]
    copy = pltpu.make_async_copy(place_ref, here_ref, sem)
    copy.start()
    copy.wait()
    per = parts * CAP
    tok = ids_ref.shape[1] // parts
    row = lax.broadcasted_iota(jnp.int32, (experts * per, tok), 0)
    expert = target(here_ref[0], row // per, experts)
    place = row % per
    for p in range(parts):
        at = slice(p * tok, (p + 1) * tok)
        _, slot, share = routes(ids_ref[:, at], expert, weight_ref[:, at])
        chosen = (slot == place % CAP) & (place // CAP == p)
        table = jnp.where(chosen, share, 0.0)
        high = table.astype(BF)
        high_ref[:, at] = high
        low_ref[:, at] = (table - high.astype(F32)).astype(BF)


def make_table(place, ids, weights, experts, parts, waits=()):
    shape = jax.ShapeDtypeStruct((experts * parts * CAP, ids.shape[1]), BF)
    return pl.pallas_call(
        functools.partial(table_kernel, experts, parts, len(waits)),
        out_shape=[shape] * 2,
        in_specs=[HBM] + [VMEM] * 2 + [ANY] * len(waits),
        out_specs=[VMEM] * 2,
        scratch_shapes=[pltpu.SMEM((1,), jnp.int32), pltpu.SemaphoreType.DMA],
        compiler_params=params(8),
        cost_estimate=cost(1e6, 1e6),
        name="table",
    )(place, ids, weights, *waits)


def combine_kernel(high_ref, low_ref, *refs):
    backs, out_ref = refs[:-1], refs[-1]
    back = jnp.concatenate([b[...].astype(F32) for b in backs], axis=0).astype(BF)
    tn = (((0,), (0,)), ((), ()))
    out_ref[...] = (dot(high_ref[...], back, tn) + dot(low_ref[...], back, tn)).astype(BF)


def combine(high, low, backs):
    tokens = high.shape[1]
    width = backs[0].shape[1]
    return pl.pallas_call(
        combine_kernel,
        out_shape=jax.ShapeDtypeStruct((tokens, width), BF),
        in_specs=[VMEM] * (2 + len(backs)),
        out_specs=VMEM,
        compiler_params=params(16),
        cost_estimate=cost(4 * high.size * width, 4 * high.size + 2 * tokens * width),
        name="combine",
    )(high, low, *backs)


def swaps(size, k):
    return [(i, i ^ k) for i in range(size)]


def sends(size, n):
    if size & (size - 1) == 0:
        return swaps(size, n)
    return [(i, (i + n) % size) for i in range(size)]


def others(a, axis, size):
    return [lax.ppermute(a, axis, [(i, (i + k) % size) for i in range(size)]) for k in range(1, size)]


def layer(
    queries,
    suffix_keys,
    suffix_values,
    prefix_keys,
    prefix_values,
    prefix_groups,
    shot_counts,
    lengths,
    hidden,
    expert_ids,
    gate_weights,
    gate_proj,
    up_proj,
    down_proj,
):
    ep, tp, pp = lax.axis_size("ep"), lax.axis_size("tp"), lax.axis_size("pp")
    local_heads = queries.shape[1] // HD
    head_group = HEADS // KVH
    kv_heads = max(1, local_heads // head_group)
    per_kv = min(local_heads, head_group)
    width = kv_heads * HD

    def head_block(tp_index):
        return (tp_index * local_heads // head_group) // kv_heads

    rows = prefix_keys.shape[0]
    ids, shares = expert_ids.T, gate_weights.T
    place = lax.axis_index("ep").reshape(1)
    fixed = dict(per_kv=per_kv, width=width, head_block=head_block)
    own = (suffix_keys, suffix_values)

    features = [hidden] + others(hidden, "pp", pp)
    pack, facts = make_pack(
        prefix_keys, prefix_values, prefix_groups, shot_counts, lengths, width, head_block
    )
    basic = (queries, facts)
    outgoing = select(place, ids, features, ep, pp)
    started = mark(outgoing[0], 1e10)
    arrived = [outgoing[0]]
    for n in reversed(range(1, ep)):
        arrived.insert(1, lax.ppermute(outgoing[n], "ep", sends(ep, n)))

    ringed = ep & (ep - 1) == 0 and rows % 128 == 0
    if ringed:
        held = [pack]
        stride = ep // 2
        while stride:
            first, *rest = held
            moved = [lax.ppermute(first, "ep", swaps(ep, stride))]
            moved += [lax.ppermute(b, "ep", swaps(ep, stride)) for b in rest]
            held += moved
            stride //= 2
        order = [0, ep // 2] + [n for n in range(1, ep) if n != ep // 2]
        chips = [[held[n]] + others(held[n], "pp", pp) for n in order[:ep]]
    else:
        every = lax.all_gather(pack, ("ep", "pp"), axis=0)
        step = max(1, 256 // rows)
        keys = every[:, :rows].reshape(-1, step * rows, width)
        values = every[:, rows : 2 * rows].reshape(-1, step * rows, width)
        lines = max(1, rows // width)
        groups = every[:, 2 * rows : 2 * rows + lines, : rows // lines].reshape(-1, step * rows // width, width)
        groups = jnp.pad(groups, ((0, 0), (0, GROUP_ROWS - groups.shape[1]), (0, 0)))
        joined = jnp.concatenate([keys, values, groups], axis=1)
        chips = [[joined[n] for n in range(joined.shape[0])]]

    partial = []

    def attend_chip(n, waits):
        last = n == len(chips) - 1
        result = attend(
            *basic, own if n == 0 else None, chips[n], partial if last else [], last, waits=waits, **fixed
        )
        if not last:
            partial.append(result)
        return (result if last else result[1],)

    turn = iter(range(len(chips)))
    wait = attend_chip(next(turn), (started,)) if len(chips) > 1 else (started,)

    mine = gateup(arrived, gate_proj, up_proj, wait)
    other = others(mine, "pp", pp)
    other = jnp.stack(other) if pp > 2 else other[0][None]
    wait = attend_chip(next(turn), (mine,)) if len(chips) > 2 else (mine,)
    parts = down(mine, other, down_proj, tp, wait)
    high, low = make_table(place, ids, shares, ep, pp, (parts[0],))
    received = []
    for n in range(1, tp):
        received.append(lax.ppermute(parts[n], "tp", sends(tp, n)))
    wait = attend_chip(next(turn), (high,)) if len(chips) > 3 else ()
    done = join([parts[0]] + received, ep, wait)
    backs = [done[0]]
    for n in reversed(range(1, ep)):
        backs.insert(1, lax.ppermute(done[n], "ep", [(t, f) for f, t in sends(ep, n)]))
    returned = mark(done[0], 1e6)
    for n in turn:
        (context,) = attend_chip(n, (returned,))
    moe_out = combine(high, low, backs)
    return (context, moe_out)


def solution(mesh):
    placed = (
        P(("grp", "ep", "pp"), "tp"),
        P(("grp", "ep", "pp"), None),
        P(("grp", "ep", "pp"), None),
        P(("grp", "ep", "pp"), None),
        P(("grp", "ep", "pp"), None),
        P(("grp", "ep", "pp")),
        P(("grp", "ep", "pp")),
        P(("grp", "ep", "pp")),
        P(("grp", "ep", "pp"), None),
        P(("grp", "ep"), None),
        P(("grp", "ep"), None),
        P("ep", "pp", "tp"),
        P("ep", "pp", "tp"),
        P("ep", "tp", "pp"),
    )
    return jax.shard_map(
        layer,
        mesh=mesh,
        in_specs=placed,
        out_specs=(P(("grp", "ep", "pp"), "tp"), P(("grp", "ep"), ("pp", "tp"))),
        check_vma=False,
    )
```

time: 153 us -> 65.2 us (0.43)
  matrix products: 46.9 us -> 0 us
  blocking collectives: 33.9 us -> 0 us
  Pallas kernels: 0 us -> 28.4 us
  other arithmetic: 19.1 us -> 0 us
  between operations: 17 us -> 2.17 us
  starting transfers between devices: 3.71 us -> 17.3 us
  local copies, waits for them, and re-layouts: 13.7 us -> 1.79 us
  waiting for transfers between devices: 17.6 us -> 15.3 us
    dot_general x9 -> x0, matrix products: 46.9 us -> none  [the longest x2 19.3 us: score_of(): jnp.einsum('tkgd,skd->tkgs', query_heads, shaped, preferred_element_type=...]
    pallas_call x0 -> x13, Pallas kernels: none -> 28.4 us  [the longest x4 20 us: attend(): pl.pallas_call(functools.partial(attend_kernel, cfg), out_shape=context i...]
    all_to_all x1 -> x0, blocking collectives: 21.7 us -> none  [shards(): lax.all_to_all(outgoing.reshape(ep_size * pp_size, CAP, half_width), ('ep...]
    psum x1 -> x0, waiting for transfers between devices: 17.5 us -> none  [shards(): lax.psum(up_part.astype(jnp.bfloat16), 'pp').astype(jnp.float32)]
    ppermute x0 -> x16, starting transfers between devices: none -> 17.3 us  [the longest x2 5.22 us: layer(): moved = [lax.ppermute(first, 'ep', swaps(ep, stride))]]
    reduce_sum x4 -> x0, other arithmetic: 16.9 us -> none  [the longest x2 16.1 us: online_update(): new_sum = run_sum * factor + jnp.sum(weights, axis=-1)]
    ppermute x0 -> x16, waiting for transfers between devices: none -> 15.3 us  [the longest x2 13 us: layer(): moved = [lax.ppermute(first, 'ep', swaps(ep, stride))]]
    all_gather x1 -> x0, blocking collectives: 12.1 us -> none  [shards(): lax.all_gather(prefix_groups, ('ep', 'pp'), axis=0, tiled=True)]
  transfers between devices with their start and end apart: 5 -> 16, of which waited for: 1 -> 4; matrix products, arithmetic and copies ran while one was open for 45% -> 0% of each run, Pallas kernels for 0% -> 42%
where the time goes in v1:
time: 65.2 us; the launch traced here: 65 us
  Pallas kernels  28.4 us (44%)
  starting transfers between devices  17.3 us (27%)
  waiting for transfers between devices  15.3 us (23%)
  between operations  2.17 us (3%)
  local copies, waits for them, and re-layouts  1.79 us (3%)
    pallas_call x4, Pallas kernels, attend(): pl.pallas_call(functools.partial(attend_kernel, cfg), out_shape=context i...  20 us
    ppermute x2, waiting for transfers between devices, layer(): moved = [lax.ppermute(first, 'ep', swaps(ep, stride))]  13 us
    ppermute x2, starting transfers between devices, layer(): moved = [lax.ppermute(first, 'ep', swaps(ep, stride))]  5.22 us
    ppermute x3, starting transfers between devices, layer(): lax.ppermute(done[n], 'ep', [(t, f) for f, t in sends(ep, n)])  4.45 us
    ppermute x3, starting transfers between devices, layer(): arrived.insert(1, lax.ppermute(outgoing[n], 'ep', sends(ep, n)))  4.39 us
    pallas_call x1, Pallas kernels, select(): pl.pallas_call(functools.partial(select_kernel, (experts, parts)), out_sh...  2.72 us
    unnamed x30, local copies, waits for them, and re-layouts  1.79 us
    pallas_call x1, Pallas kernels, make_pack(): pl.pallas_call(functools.partial(pack_kernel, width, head_block), out_sha...  1.75 us
  transfers between devices with their start and end apart: 16, of which 4 were waited for; matrix products, arithmetic and copies ran while one was open for 0% of the time, Pallas kernels for 42%

profile of v1, /device:TPU:0, one launch (start us, length us, event | category | flops | bytes accessed | tf_op | source)
XLA Modules:
  0.0 65.0 jit_solution(1505716131263727251)
XLA Ops:
  2.5 1.7 %pack.1 = (bf16[528,256]{1,0:T(8,128)(2,1)}, f32[16,128]{1,0:T(8,128)}) custom-call(bf16[256,512]{1,0:T(8,128)(2,1)} %k_ref.1, bf16[256,512]{1,0:T(8,128)(2,1)} %v_ref.1, s32[1,256]{1,0:T(1,128)} %bitcast.9, s32[1]{0:T(128)S(6)} %copy.16.shots_ref, s32[1]{0:T(128)S(6)} %copy.17.len_ref), custom_call_target="tpu_custom_call" | custom-call | bytes 1048576 | tf_op jit(solution)/shard_map/pack/pallas_call | solution.py:210
  4.2 2.6 %collective-permute-start.5 = (bf16[528,256]{1,0:T(8,128)(2,1)}, bf16[528,256]{1,0:T(8,128)(2,1)S(1)}, u32[]{:S(2)}, u32[]{:S(2)}) collective-permute-start(bf16[528,256]{1,0:T(8,128)(2,1)} %get-tuple-element.23.refs_3_), channel_id=1, source_target_pairs={{0,4},{4,0},{8,12},{12,8},{1,5},{5,1},{9,13},{13,9},{2,6},{6,2},{1... | collective-permute-start | bytes 811016 | tf_op jit(solution)/shard_map/ppermute | solution.py:500
  6.9 2.6 %collective-permute-start = (bf16[528,256]{1,0:T(8,128)(2,1)}, bf16[528,256]{1,0:T(8,128)(2,1)S(1)}, u32[]{:S(2)}, u32[]{:S(2)}) collective-permute-start(bf16[528,256]{1,0:T(8,128)(2,1)} %get-tuple-element.23.refs_3_), channel_id=1, source_target_pairs={{0,8},{4,12},{8,0},{12,4},{1,9},{5,13},{9,1},{13,5},{2,10},{6,14},... | collective-permute-start | bytes 811016 | tf_op jit(solution)/shard_map/ppermute | solution.py:500
  9.5 10.4 %collective-permute-done.5.refs_1_ = bf16[528,256]{1,0:T(8,128)(2,1)S(1)} collective-permute-done((bf16[528,256]{1,0:T(8,128)(2,1)}, bf16[528,256]{1,0:T(8,128)(2,1)S(1)}, u32[]{:S(2)}, u32[]{:S(2)}) %collective-permute-start.5) | collective-permute-done | bytes 270368 | tf_op jit(solution)/shard_map/ppermute | solution.py:500
  19.9 2.6 %collective-permute-done.refs_1_ = bf16[528,256]{1,0:T(8,128)(2,1)S(1)} collective-permute-done((bf16[528,256]{1,0:T(8,128)(2,1)}, bf16[528,256]{1,0:T(8,128)(2,1)S(1)}, u32[]{:S(2)}, u32[]{:S(2)}) %collective-permute-start) | collective-permute-done | bytes 270368 | tf_op jit(solution)/shard_map/ppermute | solution.py:500
  22.9 2.7 %select.1 = (bf16[24,2048]{1,0:T(8,128)(2,1)}, bf16[24,2048]{1,0:T(8,128)(2,1)}, bf16[24,2048]{1,0:T(8,128)(2,1)}, bf16[24,2048]{1,0:T(8,128)(2,1)}) custom-call(s32[1]{0:T(128)} %bitcast.1.place_ref, s32[8,256]{1,0:T(8,128)} %bitcast.6, bf16[128,4096]{1,0:T(8,128)(2,1)} %refs_0_.5, bf16[128,4096]{1,0:T(8,128)(2,1)} %collective-permute-done.4.refs_1_), custom_call_target="tpu_custom_call" | custom-call | flops 100663296 | bytes 1048576 | tf_op jit(solution)/shard_map/select/pallas_call | solution.py:273
  25.6 0.9 %copy-done.3 = bf16[24,2048]{1,0:T(8,128)(2,1)S(1)} copy-done((bf16[24,2048]{1,0:T(8,128)(2,1)S(1)}, bf16[24,2048]{1,0:T(8,128)(2,1)}, u32[]{:S(2)}) %copy-start.3) | copy-done | bytes 98328
  26.6 0.8 %copy-done.14 = bf16[24,2048]{1,0:T(8,128)(2,1)S(1)} copy-done((bf16[24,2048]{1,0:T(8,128)(2,1)S(1)}, bf16[24,2048]{1,0:T(8,128)(2,1)}, u32[]{:S(2)}) %copy-start.14) | copy-done | bytes 98328
  27.4 1.6 %collective-permute-start.7 = (bf16[24,2048]{1,0:T(8,128)(2,1)S(1)}, bf16[24,2048]{1,0:T(8,128)(2,1)S(1)}, u32[]{:S(2)}, u32[]{:S(2)}) collective-permute-start(bf16[24,2048]{1,0:T(8,128)(2,1)S(1)} %copy-done.14), channel_id=1, source_target_pairs={{0,4},{4,0},{8,12},{12,8},{1,5},{5,1},{9,13},{13,9},{2,6},{6,2},{1... | collective-permute-start | bytes 294920 | tf_op jit(solution)/shard_map/ppermute | solution.py:492
  29.0 1.0 %collective-permute-start.8 = (bf16[24,2048]{1,0:T(8,128)(2,1)S(1)}, bf16[24,2048]{1,0:T(8,128)(2,1)S(1)}, u32[]{:S(2)}, u32[]{:S(2)}) collective-permute-start(bf16[24,2048]{1,0:T(8,128)(2,1)S(1)} %copy-done.13), channel_id=1, source_target_pairs={{0,8},{4,12},{8,0},{12,4},{1,9},{5,13},{9,1},{13,5},{2,10},{6,14},... | collective-permute-start | bytes 294920 | tf_op jit(solution)/shard_map/ppermute | solution.py:492
  30.0 1.8 %collective-permute-start.9 = (bf16[24,2048]{1,0:T(8,128)(2,1)S(1)}, bf16[24,2048]{1,0:T(8,128)(2,1)S(1)}, u32[]{:S(2)}, u32[]{:S(2)}) collective-permute-start(bf16[24,2048]{1,0:T(8,128)(2,1)S(1)} %copy-done.12), channel_id=1, source_target_pairs={{0,12},{4,8},{8,4},{12,0},{1,13},{5,9},{9,5},{13,1},{2,14},{6,10},... | collective-permute-start | bytes 294920 | tf_op jit(solution)/shard_map/ppermute | solution.py:492
  31.9 5.7 %attend.4 = (bf16[128,4096]{1,0:T(8,128)(2,1)S(1)}, f32[128,128]{1,0:T(8,128)S(1)}) custom-call(f32[16,128]{1,0:T(8,128)S(1)} %copy-done.11, bf16[128,4096]{1,0:T(8,128)(2,1)S(1)} %copy-done.7, bf16[128,512]{1,0:T(8,128)(2,1)S(1)} %copy-done.9, bf16[128,512]{1,0:T(8,128)(2,1)S(1)} %copy-done.10, bf16[528,256]{1,0:T(8,128)(2,1)S(1)} %copy-done.8, ...), custom_call_target="tpu_custom_call" | custom-call | flops 2684354560 | bytes 2097152 | tf_op jit(solution)/shard_map/attend/pallas_call | solution.py:142
  37.6 0.9 %collective-permute-done.8.refs_2_ = bf16[24,2048]{1,0:T(8,128)(2,1)S(1)} collective-permute-done((bf16[24,2048]{1,0:T(8,128)(2,1)S(1)}, bf16[24,2048]{1,0:T(8,128)(2,1)S(1)}, u32[]{:S(2)}, u32[]{:S(2)}) %collective-permute-start.8) | collective-permute-done | bytes 98336 | tf_op jit(solution)/shard_map/ppermute | solution.py:492
  38.5 1.2 %gateup.1.refs_3_.mine_ref = bf16[96,1536]{1,0:T(8,128)(2,1)S(1)} custom-call(bf16[1,2048,768]{2,1,0:T(8,128)(2,1)S(1)} %copy-done, bf16[1,2048,768]{2,1,0:T(8,128)(2,1)S(1)} %copy-done.1, bf16[24,2048]{1,0:T(8,128)(2,1)S(1)} %copy-done.4, bf16[24,2048]{1,0:T(8,128)(2,1)S(1)} %collective-permute-done.7.refs_1_, ...), custom_call_target="tpu_custom_call" | custom-call | flops 603979776 | bytes 6291456 | tf_op jit(solution)/shard_map/gateup/pallas_call | solution.py:317
  40.3 4.0 %attend.5 = (bf16[128,4096]{1,0:T(8,128)(2,1)S(1)}, f32[128,128]{1,0:T(8,128)S(1)}) custom-call(f32[16,128]{1,0:T(8,128)S(1)} %copy-done.11, bf16[128,4096]{1,0:T(8,128)(2,1)S(1)} %copy-done.7, bf16[528,256]{1,0:T(8,128)(2,1)S(1)} %collective-permute-done.5.refs_1_, bf16[528,256]{1,0:T(8,128)(2,1)} %collective-permute-done.6.refs_2_, ...), custom_call_target="tpu_custom_call" | custom-call | flops 2147483648 | bytes 2097152 | tf_op jit(solution)/shard_map/attend/pallas_call | solution.py:142
  45.1 1.6 %collective-permute-start.12 = (bf16[96,1024]{1,0:T(8,128)(2,1)S(1)}, bf16[96,1024]{1,0:T(8,128)(2,1)S(1)}, u32[]{:S(2)}, u32[]{:S(2)}) collective-permute-start(bf16[96,1024]{1,0:T(8,128)(2,1)S(1)} %get-tuple-element.36), channel_id=1, source_target_pairs={{0,2},{2,0},{1,3},{3,1},{4,6},{6,4},{5,7},{7,5},{8,10},{10,8},{9,1... | collective-permute-start | bytes 589832 | tf_op jit(solution)/shard_map/ppermute | solution.py:539
  46.7 0.8 %table.1 = (bf16[96,256]{1,0:T(8,128)(2,1)S(1)}, bf16[96,256]{1,0:T(8,128)(2,1)S(1)}) custom-call(s32[1]{0:T(128)} %bitcast.1.place_ref, s32[8,256]{1,0:T(8,128)S(1)} %bitcast.7, f32[8,256]{1,0:T(8,128)S(1)} %bitcast.8, f32[96,1024]{1,0:T(8,128)S(1)} %get-tuple-element.32.refs_0_), custom_call_target="tpu_custom_call" | custom-call | flops 1000000 | bytes 1000000 | tf_op jit(solution)/shard_map/table/pallas_call | solution.py:404
  47.5 3.2 %attend.6 = (bf16[128,4096]{1,0:T(8,128)(2,1)S(1)}, f32[128,128]{1,0:T(8,128)S(1)}) custom-call(f32[16,128]{1,0:T(8,128)S(1)} %copy-done.11, bf16[128,4096]{1,0:T(8,128)(2,1)S(1)} %copy-done.7, bf16[528,256]{1,0:T(8,128)(2,1)S(1)} %collective-permute-done.refs_1_, bf16[528,256]{1,0:T(8,128)(2,1)S(1)} %collective-permute-done.10.refs_2_, ...), custom_call_target="tpu_custom_call" | custom-call | flops 2147483648 | bytes 2097152 | tf_op jit(solution)/shard_map/attend/pallas_call | solution.py:142
  50.7 1.5 %collective-permute-done.12.refs_1_ = bf16[96,1024]{1,0:T(8,128)(2,1)S(1)} collective-permute-done((bf16[96,1024]{1,0:T(8,128)(2,1)S(1)}, bf16[96,1024]{1,0:T(8,128)(2,1)S(1)}, u32[]{:S(2)}, u32[]{:S(2)}) %collective-permute-start.12) | collective-permute-done | bytes 196640 | tf_op jit(solution)/shard_map/ppermute | solution.py:539
  52.2 1.7 %collective-permute-start.13 = (bf16[24,1024]{1,0:T(8,128)(2,1)S(1)}, bf16[24,1024]{1,0:T(8,128)(2,1)S(1)}, u32[]{:S(2)}, u32[]{:S(2)}) collective-permute-start(bf16[24,1024]{1,0:T(8,128)(2,1)S(1)} %get-tuple-element.39), channel_id=1, source_target_pairs={{4,0},{0,4},{12,8},{8,12},{5,1},{1,5},{13,9},{9,13},{6,2},{2,6},{1... | collective-permute-start | bytes 147464 | tf_op jit(solution)/shard_map/ppermute | solution.py:544
  53.8 1.3 %collective-permute-start.14 = (bf16[24,1024]{1,0:T(8,128)(2,1)S(1)}, bf16[24,1024]{1,0:T(8,128)(2,1)S(1)}, u32[]{:S(2)}, u32[]{:S(2)}) collective-permute-start(bf16[24,1024]{1,0:T(8,128)(2,1)S(1)} %get-tuple-element.40), channel_id=1, source_target_pairs={{8,0},{12,4},{0,8},{4,12},{9,1},{13,5},{1,9},{5,13},{10,2},{14,6},... | collective-permute-start | bytes 147464 | tf_op jit(solution)/shard_map/ppermute | solution.py:544
  55.1 1.5 %collective-permute-start.15 = (bf16[24,1024]{1,0:T(8,128)(2,1)S(1)}, bf16[24,1024]{1,0:T(8,128)(2,1)S(1)}, u32[]{:S(2)}, u32[]{:S(2)}) collective-permute-start(bf16[24,1024]{1,0:T(8,128)(2,1)S(1)} %get-tuple-element.41), channel_id=1, source_target_pairs={{12,0},{8,4},{4,8},{0,12},{13,1},{9,5},{5,9},{1,13},{14,2},{10,6},... | collective-permute-start | bytes 147464 | tf_op jit(solution)/shard_map/ppermute | solution.py:544
  56.6 7.1 %attend.7 = bf16[128,4096]{1,0:T(8,128)(2,1)} custom-call(f32[16,128]{1,0:T(8,128)S(1)} %copy-done.11, bf16[128,4096]{1,0:T(8,128)(2,1)S(1)} %copy-done.7, bf16[528,256]{1,0:T(8,128)(2,1)S(1)} %collective-permute-done.1.refs_1_, bf16[528,256]{1,0:T(8,128)(2,1)S(1)} %collective-permute-done.2.refs_2_, bf16[128,4096]{1,0:T(8,128)(2,1)S(1)} %get-tuple-element.25.refs_3_, ...), custom_call_target="tpu_custom_call" | custom-call | flops 2147483648 | bytes 2097152 | tf_op jit(solution)/shard_map/attend/pallas_call | solution.py:142
  63.7 1.2 %combine.1 = bf16[256,1024]{1,0:T(8,128)(2,1)} custom-call(bf16[96,256]{1,0:T(8,128)(2,1)S(1)} %get-tuple-element.33.refs_3_.high_ref, bf16[96,256]{1,0:T(8,128)(2,1)S(1)} %get-tuple-element.38.low_ref, bf16[24,1024]{1,0:T(8,128)(2,1)S(1)} %get-tuple-element.37.wait_ref.refs_0_, bf16[24,1024]{1,0:T(8,128)(2,1)S(1)} %collective-permute-done.13.refs_1_, ...), custom_call_target="tpu_custom_call" | custom-call | flops 100663296 | bytes 622592 | tf_op jit(solution)/shard_map/combine/pallas_call | solution.py:426
  (51 shorter events, 2.5 us)
Async XLA Ops:
  0.6 22.3 %collective-permute-start.4 = (bf16[128,4096]{1,0:T(8,128)(2,1)}, bf16[128,4096]{1,0:T(8,128)(2,1)}, u32[]{:S(2)}, u32[]{:S(2)}) collective-permute-start(bf16[128,4096]{1,0:T(8,128)(2,1)} %refs_0_.5), channel_id=1, source_target_pairs={{0,1},{1,0},{2,3},{3,2},{4,5},{5,4},{6,7},{7,6},{8,9},{9,8},{10,11... | collective-permute-start | bytes 3145736 | tf_op jit(solution)/shard_map/ppermute | solution.py:448
  4.2 15.7 %collective-permute-start.5 = (bf16[528,256]{1,0:T(8,128)(2,1)}, bf16[528,256]{1,0:T(8,128)(2,1)S(1)}, u32[]{:S(2)}, u32[]{:S(2)}) collective-permute-start(bf16[528,256]{1,0:T(8,128)(2,1)} %get-tuple-element.23.refs_3_), channel_id=1, source_target_pairs={{0,4},{4,0},{8,12},{12,8},{1,5},{5,1},{9,13},{13,9},{2,6},{6,2},{1... | collective-permute-start | bytes 811016 | tf_op jit(solution)/shard_map/ppermute | solution.py:500
  6.9 15.6 %collective-permute-start = (bf16[528,256]{1,0:T(8,128)(2,1)}, bf16[528,256]{1,0:T(8,128)(2,1)S(1)}, u32[]{:S(2)}, u32[]{:S(2)}) collective-permute-start(bf16[528,256]{1,0:T(8,128)(2,1)} %get-tuple-element.23.refs_3_), channel_id=1, source_target_pairs={{0,8},{4,12},{8,0},{12,4},{1,9},{5,13},{9,1},{13,5},{2,10},{6,14},... | collective-permute-start | bytes 811016 | tf_op jit(solution)/shard_map/ppermute | solution.py:500
  9.5 20.6 %collective-permute-start.3 = (bf16[528,256]{1,0:T(8,128)(2,1)}, bf16[528,256]{1,0:T(8,128)(2,1)}, u32[]{:S(2)}, u32[]{:S(2)}) collective-permute-start(bf16[528,256]{1,0:T(8,128)(2,1)} %get-tuple-element.23.refs_3_), channel_id=1, source_target_pairs={{0,1},{1,0},{2,3},{3,2},{4,5},{5,4},{6,7},{7,6},{8,9},{9,8},{10,11... | collective-permute-start | bytes 811016 | tf_op jit(solution)/shard_map/ppermute | solution.py:448
  19.9 20.4 %collective-permute-start.6 = (bf16[528,256]{1,0:T(8,128)(2,1)S(1)}, bf16[528,256]{1,0:T(8,128)(2,1)}, u32[]{:S(2)}, u32[]{:S(2)}) collective-permute-start(bf16[528,256]{1,0:T(8,128)(2,1)S(1)} %collective-permute-done.5.refs_1_), channel_id=1, source_target_pairs={{0,1},{1,0},{2,3},{3,2},{4,5},{5,4},{6,7},{7,6},{8,9},{9,8},{10,11... | collective-permute-start | bytes 811016 | tf_op jit(solution)/shard_map/ppermute | solution.py:448
  22.4 17.8 %collective-permute-start.1 = (bf16[528,256]{1,0:T(8,128)(2,1)S(1)}, bf16[528,256]{1,0:T(8,128)(2,1)S(1)}, u32[]{:S(2)}, u32[]{:S(2)}) collective-permute-start(bf16[528,256]{1,0:T(8,128)(2,1)S(1)} %collective-permute-done.refs_1_), channel_id=1, source_target_pairs={{0,4},{4,0},{8,12},{12,8},{1,5},{5,1},{9,13},{13,9},{2,6},{6,2},{1... | collective-permute-start | bytes 811016 | tf_op jit(solution)/shard_map/ppermute | solution.py:501
  26.5 5.3 %copy-start.7 = (bf16[128,4096]{1,0:T(8,128)(2,1)S(1)}, bf16[128,4096]{1,0:T(8,128)(2,1)}, u32[]{:S(2)}) copy-start(bf16[128,4096]{1,0:T(8,128)(2,1)} %refs_0_.9) | copy-start | bytes 3145732
  26.5 5.3 %copy-start.8 = (bf16[528,256]{1,0:T(8,128)(2,1)S(1)}, bf16[528,256]{1,0:T(8,128)(2,1)}, u32[]{:S(2)}) copy-start(bf16[528,256]{1,0:T(8,128)(2,1)} %get-tuple-element.23.refs_3_) | copy-start | bytes 811012
  26.5 5.3 %copy-start.9 = (bf16[128,512]{1,0:T(8,128)(2,1)S(1)}, bf16[128,512]{1,0:T(8,128)(2,1)}, u32[]{:S(2)}) copy-start(bf16[128,512]{1,0:T(8,128)(2,1)} %refs_1_.1) | copy-start | bytes 393220
  26.5 5.3 %copy-start.10 = (bf16[128,512]{1,0:T(8,128)(2,1)S(1)}, bf16[128,512]{1,0:T(8,128)(2,1)}, u32[]{:S(2)}) copy-start(bf16[128,512]{1,0:T(8,128)(2,1)} %refs_2_.1) | copy-start | bytes 393220
  26.6 5.3 %copy-start.11 = (f32[16,128]{1,0:T(8,128)S(1)}, f32[16,128]{1,0:T(8,128)}, u32[]{:S(2)}) copy-start(f32[16,128]{1,0:T(8,128)} %get-tuple-element.22.facts_ref) | copy-start | bytes 24580
  27.4 10.2 %collective-permute-start.7 = (bf16[24,2048]{1,0:T(8,128)(2,1)S(1)}, bf16[24,2048]{1,0:T(8,128)(2,1)S(1)}, u32[]{:S(2)}, u32[]{:S(2)}) collective-permute-start(bf16[24,2048]{1,0:T(8,128)(2,1)S(1)} %copy-done.14), channel_id=1, source_target_pairs={{0,4},{4,0},{8,12},{12,8},{1,5},{5,1},{9,13},{13,9},{2,6},{6,2},{1... | collective-permute-start | bytes 294920 | tf_op jit(solution)/shard_map/ppermute | solution.py:492
  29.0 9.5 %collective-permute-start.8 = (bf16[24,2048]{1,0:T(8,128)(2,1)S(1)}, bf16[24,2048]{1,0:T(8,128)(2,1)S(1)}, u32[]{:S(2)}, u32[]{:S(2)}) collective-permute-start(bf16[24,2048]{1,0:T(8,128)(2,1)S(1)} %copy-done.13), channel_id=1, source_target_pairs={{0,8},{4,12},{8,0},{12,4},{1,9},{5,13},{9,1},{13,5},{2,10},{6,14},... | collective-permute-start | bytes 294920 | tf_op jit(solution)/shard_map/ppermute | solution.py:492
  30.0 8.4 %collective-permute-start.9 = (bf16[24,2048]{1,0:T(8,128)(2,1)S(1)}, bf16[24,2048]{1,0:T(8,128)(2,1)S(1)}, u32[]{:S(2)}, u32[]{:S(2)}) collective-permute-start(bf16[24,2048]{1,0:T(8,128)(2,1)S(1)} %copy-done.12), channel_id=1, source_target_pairs={{0,12},{4,8},{8,4},{12,0},{1,13},{5,9},{9,5},{13,1},{2,14},{6,10},... | collective-permute-start | bytes 294920 | tf_op jit(solution)/shard_map/ppermute | solution.py:492
  31.8 6.7 %copy-start = (bf16[1,2048,768]{2,1,0:T(8,128)(2,1)S(1)}, bf16[1,2048,768]{2,1,0:T(8,128)(2,1)}, u32[]{:S(2)}) copy-start(bf16[1,2048,768]{2,1,0:T(8,128)(2,1)} %gate_ref.1) | copy-start | bytes 9437188
  31.8 6.6 %copy-start.1 = (bf16[1,2048,768]{2,1,0:T(8,128)(2,1)S(1)}, bf16[1,2048,768]{2,1,0:T(8,128)(2,1)}, u32[]{:S(2)}) copy-start(bf16[1,2048,768]{2,1,0:T(8,128)(2,1)} %up_ref.1) | copy-start | bytes 9437188
  31.8 6.6 %copy-start.4 = (bf16[24,2048]{1,0:T(8,128)(2,1)S(1)}, bf16[24,2048]{1,0:T(8,128)(2,1)}, u32[]{:S(2)}) copy-start(bf16[24,2048]{1,0:T(8,128)(2,1)} %get-tuple-element.24.wait_ref.refs_0_) | copy-start | bytes 294916
  39.7 4.7 %collective-permute-start.11 = (bf16[96,1536]{1,0:T(8,128)(2,1)S(1)}, bf16[96,1536]{1,0:T(8,128)(2,1)S(1)}, u32[]{:S(2)}, u32[]{:S(2)}) collective-permute-start(bf16[96,1536]{1,0:T(8,128)(2,1)S(1)} %gateup.1.refs_3_.mine_ref), channel_id=1, source_target_pairs={{0,1},{1,0},{2,3},{3,2},{4,5},{5,4},{6,7},{7,6},{8,9},{9,8},{10,11... | collective-permute-start | bytes 884744 | tf_op jit(solution)/shard_map/ppermute | solution.py:448
  39.8 7.7 %collective-permute-start.10 = (bf16[528,256]{1,0:T(8,128)(2,1)S(1)}, bf16[528,256]{1,0:T(8,128)(2,1)S(1)}, u32[]{:S(2)}, u32[]{:S(2)}) collective-permute-start(bf16[528,256]{1,0:T(8,128)(2,1)S(1)} %collective-permute-done.refs_1_), channel_id=1, source_target_pairs={{0,1},{1,0},{2,3},{3,2},{4,5},{5,4},{6,7},{7,6},{8,9},{9,8},{10,11... | collective-permute-start | bytes 811016 | tf_op jit(solution)/shard_map/ppermute | solution.py:448
  40.3 16.4 %collective-permute-start.2 = (bf16[528,256]{1,0:T(8,128)(2,1)S(1)}, bf16[528,256]{1,0:T(8,128)(2,1)S(1)}, u32[]{:S(2)}, u32[]{:S(2)}) collective-permute-start(bf16[528,256]{1,0:T(8,128)(2,1)S(1)} %collective-permute-done.1.refs_1_), channel_id=1, source_target_pairs={{0,1},{1,0},{2,3},{3,2},{4,5},{5,4},{6,7},{7,6},{8,9},{9,8},{10,11... | collective-permute-start | bytes 811016 | tf_op jit(solution)/shard_map/ppermute | solution.py:448
  45.1 7.0 %collective-permute-start.12 = (bf16[96,1024]{1,0:T(8,128)(2,1)S(1)}, bf16[96,1024]{1,0:T(8,128)(2,1)S(1)}, u32[]{:S(2)}, u32[]{:S(2)}) collective-permute-start(bf16[96,1024]{1,0:T(8,128)(2,1)S(1)} %get-tuple-element.36), channel_id=1, source_target_pairs={{0,2},{2,0},{1,3},{3,1},{4,6},{6,4},{5,7},{7,5},{8,10},{10,8},{9,1... | collective-permute-start | bytes 589832 | tf_op jit(solution)/shard_map/ppermute | solution.py:539
  52.2 11.5 %collective-permute-start.13 = (bf16[24,1024]{1,0:T(8,128)(2,1)S(1)}, bf16[24,1024]{1,0:T(8,128)(2,1)S(1)}, u32[]{:S(2)}, u32[]{:S(2)}) collective-permute-start(bf16[24,1024]{1,0:T(8,128)(2,1)S(1)} %get-tuple-element.39), channel_id=1, source_target_pairs={{4,0},{0,4},{12,8},{8,12},{5,1},{1,5},{13,9},{9,13},{6,2},{2,6},{1... | collective-permute-start | bytes 147464 | tf_op jit(solution)/shard_map/ppermute | solution.py:544
  53.8 9.9 %collective-permute-start.14 = (bf16[24,1024]{1,0:T(8,128)(2,1)S(1)}, bf16[24,1024]{1,0:T(8,128)(2,1)S(1)}, u32[]{:S(2)}, u32[]{:S(2)}) collective-permute-start(bf16[24,1024]{1,0:T(8,128)(2,1)S(1)} %get-tuple-element.40), channel_id=1, source_target_pairs={{8,0},{12,4},{0,8},{4,12},{9,1},{13,5},{1,9},{5,13},{10,2},{14,6},... | collective-permute-start | bytes 147464 | tf_op jit(solution)/shard_map/ppermute | solution.py:544
  55.1 8.6 %collective-permute-start.15 = (bf16[24,1024]{1,0:T(8,128)(2,1)S(1)}, bf16[24,1024]{1,0:T(8,128)(2,1)S(1)}, u32[]{:S(2)}, u32[]{:S(2)}) collective-permute-start(bf16[24,1024]{1,0:T(8,128)(2,1)S(1)} %get-tuple-element.41), channel_id=1, source_target_pairs={{12,0},{8,4},{4,8},{0,12},{13,1},{9,5},{5,9},{1,13},{14,2},{10,6},... | collective-permute-start | bytes 147464 | tf_op jit(solution)/shard_map/ppermute | solution.py:544
  (7 other events, 17.1 us)

commit v2 on v1

--- a/solution.py
+++ b/solution.py
@@ -21,7 +21,6 @@
 STACK = 2
 ATT_MIB = 24
 VMEM_ALL = 67043328
-SELECT_KIB = 960
 
 
 BF = jnp.bfloat16
@@ -60,10 +59,11 @@
     lane = lax.broadcasted_iota(jnp.int32, (tok, 128), 1)
     live = lax.broadcasted_iota(jnp.int32, (tok, HD), 0).astype(F32) < length
     if last:
-        (ctx_ref,) = refs
+        out_ref, ctx_ref, lse_ref, store_ref, sem = refs
     else:
         ctx_ref, lse_ref = refs
-        lse_ref[...] = jnp.zeros((tok, 128), F32)
+    lse_ref[...] = jnp.zeros((tok, 128), F32)
+    stores = []
     for kv in range(local_heads // per_kv):
         col = slice(kv * HD, (kv + 1) * HD)
         blocks = []
@@ -103,28 +103,38 @@
             for i, at in enumerate(ats):
                 r = slice(i * tok, (i + 1) * tok)
                 top, total = update[r, :HD], update[r, HD:]
-                mine = jnp.broadcast_to(peak[r], (tok, HD))
-                if not last:
-                    ctx_ref[:, at] = (top / total).astype(BF)
-                    level = mine + jnp.log2(total)
-                    lse_ref[...] = jnp.where(lane == base + i, level, lse_ref[...])
-                    continue
-                bound, levels = mine, []
-                for _, lse in before:
-                    level = jnp.broadcast_to(lse[:, base + i : base + i + 1], (tok, HD))
-                    levels.append(level)
-                    bound = jnp.maximum(bound, level)
-                if before:
-                    factor = jnp.exp2(mine - bound)
-                    top, total = top * factor, total * factor
-                for (ctx, _), level in zip(before, levels):
-                    factor = jnp.exp2(level - bound)
-                    top = top + ctx[:, at].astype(F32) * factor
-                    total = total + factor
-                ctx_ref[:, at] = jnp.where(live, top / total, 0.0).astype(BF)
+                ctx_ref[:, at] = (top / total).astype(BF)
+                level = jnp.broadcast_to(peak[r], (tok, HD)) + jnp.log2(total)
+                lse_ref[...] = jnp.where(lane == base + i, level, lse_ref[...])
 
         for i in range(0, per_kv, stack):
             group(kv * per_kv + i)
+        if not before and not last:
+            continue
+        levels = [lse_ref[...]] + [lse[...] for _, lse in before]
+        bound = functools.reduce(jnp.maximum, levels)
+        factors = [jnp.exp2(level - bound) for level in levels]
+        total = functools.reduce(jnp.add, factors)
+        shares = [factor / total for factor in factors[1:]]
+        for h in range(kv * per_kv, (kv + 1) * per_kv):
+            at = slice(h * HD, (h + 1) * HD)
+            mine = ctx_ref[:, at].astype(F32)
+            result = mine
+            for (ctx, _), share in zip(before, shares):
+                share = jnp.broadcast_to(share[:, h : h + 1], (tok, HD))
+                result = result + (ctx[:, at].astype(F32) - mine) * share
+            if last:
+                store_ref[:, at] = jnp.where(live, result, 0.0).astype(BF)
+            else:
+                ctx_ref[:, at] = result.astype(BF)
+        if last:
+            at = slice(kv * per_kv * HD, (kv + 1) * per_kv * HD)
+            stores.append(pltpu.make_async_copy(store_ref.at[:, at], out_ref.at[:, at], sem.at[kv]))
+            stores[-1].start()
+        elif kv == local_heads // per_kv - 1:
+            lse_ref[...] = bound + jnp.log2(total)
+    for store in stores:
+        store.wait()
 
 
 def attend(queries, facts, own, packs, before, last, per_kv, width, head_block, waits=()):
@@ -139,11 +149,16 @@
     context = jax.ShapeDtypeStruct((tok, columns), BF)
     level = jax.ShapeDtypeStruct((tok, 128), F32)
     keys = sum(rows_of) + (tok if first else 0)
+    scratch = []
+    if last:
+        scratch = [pltpu.VMEM((tok, columns), BF), pltpu.VMEM((tok, 128), F32), pltpu.VMEM((tok, columns), BF)]
+        scratch.append(pltpu.SemaphoreType.DMA((max(1, local_heads // per_kv),)))
     return pl.pallas_call(
         functools.partial(attend_kernel, cfg),
         out_shape=context if last else [context, level],
         in_specs=[VMEM] * len(operands) + [ANY] * len(waits),
-        out_specs=VMEM if last else [VMEM, VMEM],
+        out_specs=HBM if last else [VMEM, VMEM],
+        scratch_shapes=scratch,
         compiler_params=params(ATT_MIB),
         cost_estimate=cost(8 * tok * local_heads * keys * HD, 4 * tok * columns),
         name="attend",
@@ -169,24 +184,15 @@
     return taken, slot, share
 
 
-def pack_kernel(width, head_block, k_ref, v_ref, g_ref, shots_ref, len_ref, out_ref, facts_ref, *scratch):
-    groups_ref, held_ref, line_ref, one_ref, two_ref, sem = scratch
+def pack_kernel(width, head_block, k_ref, v_ref, g_ref, out_ref, groups_ref, held_ref, sem):
     rows = k_ref.shape[0]
     first = pl.multiple_of(head_block(lax.axis_index("tp")) * width, 128)
     copies = [pltpu.make_async_copy(g_ref, groups_ref, sem.at[2])]
     for n, ref in enumerate((k_ref, v_ref)):
         place = held_ref.at[n * rows : (n + 1) * rows, :]
         copies.append(pltpu.make_async_copy(ref.at[:, pl.ds(first, width)], place, sem.at[n]))
-    copies.append(pltpu.make_async_copy(shots_ref, one_ref, sem.at[4]))
-    copies.append(pltpu.make_async_copy(len_ref, two_ref, sem.at[5]))
     for copy in copies:
         copy.start()
-    copies[3].wait()
-    copies[4].wait()
-    line_ref[0:8, :] = jnp.full((8, 128), one_ref[0].astype(F32))
-    line_ref[8:16, :] = jnp.full((8, 128), two_ref[0].astype(F32))
-    facts = pltpu.make_async_copy(line_ref, facts_ref, sem.at[4])
-    facts.start()
     copies[0].wait()
     groups = groups_ref[...].astype(F32)
     pad = jnp.full((GROUP_ROWS - groups.shape[0], groups.shape[1]), 0.0, F32)
@@ -199,31 +205,27 @@
     copies[2].wait()
     store = pltpu.make_async_copy(held_ref, out_ref, sem.at[3])
     store.start()
-    facts.wait()
     store.wait()
 
 
-def make_pack(keys, values, groups, shots, lengths, width, head_block):
+def make_pack(keys, values, groups, width, head_block):
     rows = keys.shape[0]
     lines = max(1, rows // width)
     shape = (2 * rows + GROUP_ROWS, width)
     return pl.pallas_call(
         functools.partial(pack_kernel, width, head_block),
-        out_shape=[jax.ShapeDtypeStruct(shape, BF), jax.ShapeDtypeStruct((16, 128), F32)],
-        in_specs=[HBM] * 5,
-        out_specs=[HBM] * 2,
+        out_shape=jax.ShapeDtypeStruct(shape, BF),
+        in_specs=[HBM] * 3,
+        out_specs=HBM,
         scratch_shapes=[
             pltpu.VMEM((lines, rows // lines), jnp.int32),
             pltpu.VMEM(shape, BF),
-            pltpu.VMEM((16, 128), F32),
-            pltpu.SMEM((1,), jnp.int32),
-            pltpu.SMEM((1,), jnp.int32),
-            pltpu.SemaphoreType.DMA((6,)),
+            pltpu.SemaphoreType.DMA((4,)),
         ],
         compiler_params=pltpu.CompilerParams(vmem_limit_bytes=VMEM_ALL),
         cost_estimate=cost(0, 4 * rows * width * 4),
         name="pack",
-    )(keys, values, groups.reshape(lines, rows // lines), shots, lengths)
+    )(keys, values, groups.reshape(lines, rows // lines))
 
 
 def target(me, n, size):
@@ -232,8 +234,8 @@
 
 def select_kernel(cfg, place_ref, ids_ref, *refs):
     experts, parts = cfg
-    hidden, outs = refs[:parts], refs[parts : parts + experts]
-    own_ref, held_ref, here_ref, sem = refs[parts + experts :]
+    hidden, outs = refs[:parts], refs[parts + 1 : parts + 1 + experts]
+    own_ref, held_ref, here_ref, sem = refs[parts + 1 + experts :]
     tok, model = hidden[0].shape
     half = model // parts
     me = lax.axis_index("pp")
@@ -267,13 +269,13 @@
         outs[e][...] = dot(pick[e * per : (e + 1) * per, :].astype(BF), held_ref[...]).astype(BF)
 
 
-def select(place, ids, hidden, experts, parts):
+def select(place, ids, hidden, experts, parts, wait):
     tok, model = hidden[0].shape
     half = model // parts
     return pl.pallas_call(
         functools.partial(select_kernel, (experts, parts)),
         out_shape=[jax.ShapeDtypeStruct((parts * CAP, half), BF)] * experts,
-        in_specs=[HBM] * (2 + parts),
+        in_specs=[HBM] * (2 + parts) + [ANY],
         out_specs=[VMEM] * experts,
         scratch_shapes=[
             pltpu.VMEM(ids.shape, jnp.int32),
@@ -281,26 +283,26 @@
             pltpu.SMEM((1,), jnp.int32),
             pltpu.SemaphoreType.DMA((2 + parts,)),
         ],
-        compiler_params=pltpu.CompilerParams(vmem_limit_bytes=VMEM_ALL - (SELECT_KIB << 10)),
-        cost_estimate=cost(4 * tok * model * experts * CAP, 2 * tok * model),
+        compiler_params=params(16),
+        cost_estimate=cost(1e10, 2 * tok * model),
         name="select",
-    )(place, ids, *hidden)
-
-
-def mark_kernel(wait_ref, out_ref):
-    out_ref[...] = jnp.zeros_like(out_ref)
-
-
-def mark(wait, flops):
+    )(place, ids, *hidden, wait)
+
+
+def mark_kernel(*refs):
+    refs[-1][...] = jnp.zeros_like(refs[-1])
+
+
+def mark(flops, *waits):
     return pl.pallas_call(
         mark_kernel,
         out_shape=jax.ShapeDtypeStruct((8, 128), F32),
-        in_specs=[ANY],
+        in_specs=[ANY] * len(waits),
         out_specs=VMEM,
         compiler_params=params(1),
         cost_estimate=cost(flops, 4096),
         name="mark",
-    )(wait)
+    )(*waits)
 
 
 def gateup_kernel(pieces, waits, gate_ref, up_ref, *refs):
@@ -481,12 +483,12 @@
     own = (suffix_keys, suffix_values)
 
     features = [hidden] + others(hidden, "pp", pp)
-    pack, facts = make_pack(
-        prefix_keys, prefix_values, prefix_groups, shot_counts, lengths, width, head_block
-    )
+    pack = make_pack(prefix_keys, prefix_values, prefix_groups, width, head_block)
+    line = lax.broadcasted_iota(jnp.int32, (16, 128), 0)
+    facts = jnp.where(line < 8, shot_counts[:, None], lengths[:, None]).astype(F32)
     basic = (queries, facts)
-    outgoing = select(place, ids, features, ep, pp)
-    started = mark(outgoing[0], 1e10)
+    packed = mark(1e10)
+    outgoing = select(place, ids, features, ep, pp, packed)
     arrived = [outgoing[0]]
     for n in reversed(range(1, ep)):
         arrived.insert(1, lax.ppermute(outgoing[n], "ep", sends(ep, n)))
@@ -502,7 +504,9 @@
             held += moved
             stride //= 2
         order = [0, ep // 2] + [n for n in range(1, ep) if n != ep // 2]
-        chips = [[held[n]] + others(held[n], "pp", pp) for n in order[:ep]]
+        chips = []
+        for n in order[:ep]:
+            chips.append([held[n]] + others(held[n], "pp", pp))
     else:
         every = lax.all_gather(pack, ("ep", "pp"), axis=0)
         step = max(1, 256 // rows)
@@ -518,33 +522,34 @@
 
     def attend_chip(n, waits):
         last = n == len(chips) - 1
-        result = attend(
-            *basic, own if n == 0 else None, chips[n], partial if last else [], last, waits=waits, **fixed
-        )
+        before = partial if last or n == 1 else []
+        result = attend(*basic, own if n == 0 else None, chips[n], before, last, waits=waits, **fixed)
         if not last:
-            partial.append(result)
+            partial[:] = [result] if n == 1 else partial + [result]
         return (result if last else result[1],)
 
     turn = iter(range(len(chips)))
-    wait = attend_chip(next(turn), (started,)) if len(chips) > 1 else (started,)
+    wait = attend_chip(next(turn), (outgoing[0],)) if len(chips) > 1 else (outgoing[0],)
+    wait = attend_chip(next(turn), wait) if len(chips) > 2 else wait
 
     mine = gateup(arrived, gate_proj, up_proj, wait)
     other = others(mine, "pp", pp)
     other = jnp.stack(other) if pp > 2 else other[0][None]
-    wait = attend_chip(next(turn), (mine,)) if len(chips) > 2 else (mine,)
-    parts = down(mine, other, down_proj, tp, wait)
-    high, low = make_table(place, ids, shares, ep, pp, (parts[0],))
+    high, low = make_table(place, ids, shares, ep, pp, (mine,))
+    parts = down(mine, other, down_proj, tp, (high,))
     received = []
     for n in range(1, tp):
         received.append(lax.ppermute(parts[n], "tp", sends(tp, n)))
-    wait = attend_chip(next(turn), (high,)) if len(chips) > 3 else ()
+    wait = (mark(1e6, parts[0]),)
+    wait = attend_chip(next(turn), wait) if len(chips) > 3 else wait
     done = join([parts[0]] + received, ep, wait)
     backs = [done[0]]
     for n in reversed(range(1, ep)):
         backs.insert(1, lax.ppermute(done[n], "ep", [(t, f) for f, t in sends(ep, n)]))
-    returned = mark(done[0], 1e6)
+    wait = (mark(1e6, done[0]),)
     for n in turn:
-        (context,) = attend_chip(n, (returned,))
+        wait = attend_chip(n, wait)
+    (context,) = wait
     moe_out = combine(high, low, backs)
     return (context, moe_out)
 

time: 65.2 us -> 57.3 us (0.88)
  Pallas kernels: 28.4 us -> 24.2 us
  waiting for transfers between devices: 15.3 us -> 12.2 us
  local copies, waits for them, and re-layouts: 1.79 us -> 0.13 us
  starting transfers between devices: 17.3 us -> 18.4 us
    ppermute x2, waiting for transfers between devices: 13 us -> 9.19 us  [layer(): moved = [lax.ppermute(first, 'ep', swaps(ep, stride))]]
    pallas_call x4, Pallas kernels: 20 us -> 17 us  [attend(): pl.pallas_call(functools.partial(attend_kernel, cfg), out_shape=context i...]
    unnamed x30 -> x20, local copies, waits for them, and re-layouts: 1.79 us -> 0.06 us
    pallas_call x1, Pallas kernels: 2.72 us -> 1.62 us  [select(): pl.pallas_call(functools.partial(select_kernel, (experts, parts)), out_sh...]
    ppermute x1, waiting for transfers between devices: 1.46 us -> 2.32 us  [layer(): received.append(lax.ppermute(parts[n], 'tp', sends(tp, n)))]
  transfers between devices with their start and end apart: 16 -> 16, of which waited for: 4 -> 4; matrix products, arithmetic and copies ran while one was open for 0% -> 0% of each run, Pallas kernels for 42% -> 37%
where the time goes in v2:
time: 57.3 us; the launch traced here: 57.1 us
  Pallas kernels  24.2 us (42%)
  starting transfers between devices  18.4 us (32%)
  waiting for transfers between devices  12.2 us (21%)
  between operations  2.17 us (4%)
    pallas_call x4, Pallas kernels, attend(): pl.pallas_call(functools.partial(attend_kernel, cfg), out_shape=context i...  17 us
    ppermute x2, waiting for transfers between devices, layer(): moved = [lax.ppermute(first, 'ep', swaps(ep, stride))]  9.19 us
    ppermute x2, starting transfers between devices, layer(): moved = [lax.ppermute(first, 'ep', swaps(ep, stride))]  5.71 us
    ppermute x3, starting transfers between devices, layer(): arrived.insert(1, lax.ppermute(outgoing[n], 'ep', sends(ep, n)))  4.8 us
    ppermute x3, starting transfers between devices, layer(): lax.ppermute(done[n], 'ep', [(t, f) for f, t in sends(ep, n)])  4.45 us
    ppermute x1, waiting for transfers between devices, layer(): received.append(lax.ppermute(parts[n], 'tp', sends(tp, n)))  2.32 us
    pallas_call x1, Pallas kernels, make_pack(): pl.pallas_call(functools.partial(pack_kernel, width, head_block), out_sha...  1.73 us
    pallas_call x1, Pallas kernels, select(): pl.pallas_call(functools.partial(select_kernel, (experts, parts)), out_sh...  1.62 us
  transfers between devices with their start and end apart: 16, of which 4 were waited for; matrix products, arithmetic and copies ran while one was open for 0% of the time, Pallas kernels for 37%

profile of v2, /device:TPU:0, one launch (start us, length us, event | category | flops | bytes accessed | tf_op | source)
XLA Modules:
  0.0 57.1 jit_solution(9341472107932764959)
XLA Ops:
  0.6 1.7 %pack.1.refs_3_ = bf16[528,256]{1,0:T(8,128)(2,1)} custom-call(bf16[256,512]{1,0:T(8,128)(2,1)} %k_ref.1, bf16[256,512]{1,0:T(8,128)(2,1)} %v_ref.1, s32[1,256]{1,0:T(1,128)} %bitcast.13), custom_call_target="tpu_custom_call" | custom-call | bytes 1048576 | tf_op jit(solution)/shard_map/pack/pallas_call | solution.py:215
  2.4 4.1 %collective-permute-start = (bf16[528,256]{1,0:T(8,128)(2,1)}, bf16[528,256]{1,0:T(8,128)(2,1)S(1)}, u32[]{:S(2)}, u32[]{:S(2)}) collective-permute-start(bf16[528,256]{1,0:T(8,128)(2,1)} %pack.1.refs_3_), channel_id=1, source_target_pairs={{0,8},{4,12},{8,0},{12,4},{1,9},{5,13},{9,1},{13,5},{2,10},{6,14},... | collective-permute-start | bytes 811016 | tf_op jit(solution)/shard_map/ppermute | solution.py:502
  6.5 1.6 %collective-permute-start.3 = (bf16[528,256]{1,0:T(8,128)(2,1)}, bf16[528,256]{1,0:T(8,128)(2,1)S(1)}, u32[]{:S(2)}, u32[]{:S(2)}) collective-permute-start(bf16[528,256]{1,0:T(8,128)(2,1)} %pack.1.refs_3_), channel_id=1, source_target_pairs={{0,4},{4,0},{8,12},{12,8},{1,5},{5,1},{9,13},{13,9},{2,6},{6,2},{1... | collective-permute-start | bytes 811016 | tf_op jit(solution)/shard_map/ppermute | solution.py:502
  8.1 0.5 collective-permute-start.6
  9.9 9.2 %collective-permute-done.refs_1_ = bf16[528,256]{1,0:T(8,128)(2,1)S(1)} collective-permute-done((bf16[528,256]{1,0:T(8,128)(2,1)}, bf16[528,256]{1,0:T(8,128)(2,1)S(1)}, u32[]{:S(2)}, u32[]{:S(2)}) %collective-permute-start) | collective-permute-done | bytes 270368 | tf_op jit(solution)/shard_map/ppermute | solution.py:502
  19.1 0.7 %collective-permute-start.1 = (bf16[528,256]{1,0:T(8,128)(2,1)S(1)}, bf16[528,256]{1,0:T(8,128)(2,1)S(1)}, u32[]{:S(2)}, u32[]{:S(2)}) collective-permute-start(bf16[528,256]{1,0:T(8,128)(2,1)S(1)} %collective-permute-done.refs_1_), channel_id=1, source_target_pairs={{0,4},{4,0},{8,12},{12,8},{1,5},{5,1},{9,13},{13,9},{2,6},{6,2},{1... | collective-permute-start | bytes 811016 | tf_op jit(solution)/shard_map/ppermute | solution.py:503
  19.9 1.6 %select.1 = (bf16[24,2048]{1,0:T(8,128)(2,1)S(1)}, bf16[24,2048]{1,0:T(8,128)(2,1)S(1)}, bf16[24,2048]{1,0:T(8,128)(2,1)S(1)}, bf16[24,2048]{1,0:T(8,128)(2,1)S(1)}) custom-call(s32[1]{0:T(128)} %bitcast.3.place_ref, s32[8,256]{1,0:T(8,128)S(1)} %bitcast.10, bf16[128,4096]{1,0:T(8,128)(2,1)S(1)} %copy-done.6, ...), custom_call_target="tpu_custom_call" | custom-call | flops 10000000000 | bytes 1048576 | tf_op jit(solution)/shard_map/select/pallas_call | solution.py:275
  21.5 1.4 %collective-permute-start.8 = (bf16[24,2048]{1,0:T(8,128)(2,1)S(1)}, bf16[24,2048]{1,0:T(8,128)(2,1)S(1)}, u32[]{:S(2)}, u32[]{:S(2)}) collective-permute-start(bf16[24,2048]{1,0:T(8,128)(2,1)S(1)} %get-tuple-element.25), channel_id=1, source_target_pairs={{0,4},{4,0},{8,12},{12,8},{1,5},{5,1},{9,13},{13,9},{2,6},{6,2},{1... | collective-permute-start | bytes 294920 | tf_op jit(solution)/shard_map/ppermute | solution.py:494
  22.9 2.1 %collective-permute-start.9 = (bf16[24,2048]{1,0:T(8,128)(2,1)S(1)}, bf16[24,2048]{1,0:T(8,128)(2,1)S(1)}, u32[]{:S(2)}, u32[]{:S(2)}) collective-permute-start(bf16[24,2048]{1,0:T(8,128)(2,1)S(1)} %get-tuple-element.26), channel_id=1, source_target_pairs={{0,8},{4,12},{8,0},{12,4},{1,9},{5,13},{9,1},{13,5},{2,10},{6,14},... | collective-permute-start | bytes 294920 | tf_op jit(solution)/shard_map/ppermute | solution.py:494
  25.0 1.4 %collective-permute-start.10 = (bf16[24,2048]{1,0:T(8,128)(2,1)S(1)}, bf16[24,2048]{1,0:T(8,128)(2,1)S(1)}, u32[]{:S(2)}, u32[]{:S(2)}) collective-permute-start(bf16[24,2048]{1,0:T(8,128)(2,1)S(1)} %get-tuple-element.27), channel_id=1, source_target_pairs={{0,12},{4,8},{8,4},{12,0},{1,13},{5,9},{9,5},{13,1},{2,14},{6,10},... | collective-permute-start | bytes 294920 | tf_op jit(solution)/shard_map/ppermute | solution.py:494
  26.4 4.7 %attend.4 = (bf16[128,4096]{1,0:T(8,128)(2,1)S(1)}, f32[128,128]{1,0:T(8,128)S(1)}) custom-call(f32[16,128]{1,0:T(8,128)S(1)} %iota.7.facts_ref, bf16[128,4096]{1,0:T(8,128)(2,1)S(1)} %copy-done.7, bf16[128,512]{1,0:T(8,128)(2,1)S(1)} %copy-done.8, bf16[128,512]{1,0:T(8,128)(2,1)S(1)} %copy-done.9, bf16[528,256]{1,0:T(8,128)(2,1)S(1)} %copy-done.3, ...), custom_call_target="tpu_custom_call" | custom-call | flops 2684354560 | bytes 2097152 | tf_op jit(solution)/shard_map/attend/pallas_call | solution.py:156
  31.1 3.9 %attend.5 = (bf16[128,4096]{1,0:T(8,128)(2,1)S(1)}, f32[128,128]{1,0:T(8,128)S(1)}) custom-call(f32[16,128]{1,0:T(8,128)S(1)} %iota.7.facts_ref, bf16[128,4096]{1,0:T(8,128)(2,1)S(1)} %copy-done.7, bf16[528,256]{1,0:T(8,128)(2,1)S(1)} %collective-permute-done.3.refs_1_, bf16[528,256]{1,0:T(8,128)(2,1)S(1)} %collective-permute-done.4.refs_2_, ...), custom_call_target="tpu_custom_call" | custom-call | flops 2147483648 | bytes 2097152 | tf_op jit(solution)/shard_map/attend/pallas_call | solution.py:156
  35.1 0.5 collective-permute-done.10.refs_3_
  35.5 1.1 %gateup.1.refs_0_.mine_ref = bf16[96,1536]{1,0:T(8,128)(2,1)S(1)} custom-call(bf16[1,2048,768]{2,1,0:T(8,128)(2,1)S(1)} %copy-done, bf16[1,2048,768]{2,1,0:T(8,128)(2,1)S(1)} %copy-done.1, bf16[24,2048]{1,0:T(8,128)(2,1)S(1)} %get-tuple-element.20.refs_5_.refs_0_, bf16[24,2048]{1,0:T(8,128)(2,1)S(1)} %collective-permute-done.8.refs_1_, ...), custom_call_target="tpu_custom_call" | custom-call | flops 603979776 | bytes 6291456 | tf_op jit(solution)/shard_map/gateup/pallas_call | solution.py:319
  36.8 0.5 collective-permute-start.7
  37.3 0.8 %table.1 = (bf16[96,256]{1,0:T(8,128)(2,1)S(1)}, bf16[96,256]{1,0:T(8,128)(2,1)S(1)}) custom-call(s32[1]{0:T(128)} %bitcast.3.place_ref, s32[8,256]{1,0:T(8,128)S(1)} %bitcast.11, f32[8,256]{1,0:T(8,128)S(1)} %bitcast.12, bf16[96,1536]{1,0:T(8,128)(2,1)S(1)} %gateup.1.refs_0_.mine_ref), custom_call_target="tpu_custom_call" | custom-call | flops 1000000 | bytes 1000000 | tf_op jit(solution)/shard_map/table/pallas_call | solution.py:406
  38.3 0.7 %down.1 = (f32[96,1024]{1,0:T(8,128)S(1)}, bf16[96,1024]{1,0:T(8,128)(2,1)S(1)}) custom-call(bf16[96,1536]{1,0:T(8,128)(2,1)S(1)} %gateup.1.refs_0_.mine_ref, bf16[1,96,1536]{2,1,0:T(8,128)(2,1)S(1)} %bitcast.9, bf16[1,768,2048]{2,1,0:T(8,128)(2,1)S(1)} %copy-done.2, bf16[96,256]{1,0:T(8,128)(2,1)S(1)} %get-tuple-element.28.outs_0_.high_ref), custom_call_target="tpu_custom_call" | custom-call | flops 301989888 | bytes 3145728 | tf_op jit(solution)/shard_map/down/pallas_call | solution.py:349
  39.0 1.6 %collective-permute-start.12 = (bf16[96,1024]{1,0:T(8,128)(2,1)S(1)}, bf16[96,1024]{1,0:T(8,128)(2,1)S(1)}, u32[]{:S(2)}, u32[]{:S(2)}) collective-permute-start(bf16[96,1024]{1,0:T(8,128)(2,1)S(1)} %get-tuple-element.32), channel_id=1, source_target_pairs={{0,2},{2,0},{1,3},{3,1},{4,6},{6,4},{5,7},{7,5},{8,10},{10,8},{9,1... | collective-permute-start | bytes 589832 | tf_op jit(solution)/shard_map/ppermute | solution.py:542
  40.6 3.2 %attend.6 = (bf16[128,4096]{1,0:T(8,128)(2,1)S(1)}, f32[128,128]{1,0:T(8,128)S(1)}) custom-call(f32[16,128]{1,0:T(8,128)S(1)} %iota.7.facts_ref, bf16[128,4096]{1,0:T(8,128)(2,1)S(1)} %copy-done.7, bf16[528,256]{1,0:T(8,128)(2,1)S(1)} %collective-permute-done.refs_1_, bf16[528,256]{1,0:T(8,128)(2,1)S(1)} %collective-permute-done.7.refs_2_, ...), custom_call_target="tpu_custom_call" | custom-call | flops 2147483648 | bytes 2097152 | tf_op jit(solution)/shard_map/attend/pallas_call | solution.py:156
  43.8 2.3 %collective-permute-done.12.refs_1_ = bf16[96,1024]{1,0:T(8,128)(2,1)S(1)} collective-permute-done((bf16[96,1024]{1,0:T(8,128)(2,1)S(1)}, bf16[96,1024]{1,0:T(8,128)(2,1)S(1)}, u32[]{:S(2)}, u32[]{:S(2)}) %collective-permute-start.12) | collective-permute-done | bytes 196640 | tf_op jit(solution)/shard_map/ppermute | solution.py:542
  46.4 2.4 %collective-permute-start.14 = (bf16[24,1024]{1,0:T(8,128)(2,1)S(1)}, bf16[24,1024]{1,0:T(8,128)(2,1)S(1)}, u32[]{:S(2)}, u32[]{:S(2)}) collective-permute-start(bf16[24,1024]{1,0:T(8,128)(2,1)S(1)} %get-tuple-element.36), channel_id=1, source_target_pairs={{8,0},{12,4},{0,8},{4,12},{9,1},{13,5},{1,9},{5,13},{10,2},{14,6},... | collective-permute-start | bytes 147464 | tf_op jit(solution)/shard_map/ppermute | solution.py:548
  48.8 1.8 %collective-permute-start.15 = (bf16[24,1024]{1,0:T(8,128)(2,1)S(1)}, bf16[24,1024]{1,0:T(8,128)(2,1)S(1)}, u32[]{:S(2)}, u32[]{:S(2)}) collective-permute-start(bf16[24,1024]{1,0:T(8,128)(2,1)S(1)} %get-tuple-element.37), channel_id=1, source_target_pairs={{12,0},{8,4},{4,8},{0,12},{13,1},{9,5},{5,9},{1,13},{14,2},{10,6},... | collective-permute-start | bytes 147464 | tf_op jit(solution)/shard_map/ppermute | solution.py:548
  50.6 5.2 %attend.7 = bf16[128,4096]{1,0:T(8,128)(2,1)} custom-call(f32[16,128]{1,0:T(8,128)S(1)} %iota.7.facts_ref, bf16[128,4096]{1,0:T(8,128)(2,1)S(1)} %copy-done.7, bf16[528,256]{1,0:T(8,128)(2,1)S(1)} %collective-permute-done.1.refs_1_, bf16[528,256]{1,0:T(8,128)(2,1)S(1)} %collective-permute-done.2.refs_2_, bf16[128,4096]{1,0:T(8,128)(2,1)S(1)} %get-tuple-element.23.refs_3_, ...), custom_call_target="tpu_custom_call" | custom-call | flops 2147483648 | bytes 2097152 | tf_op jit(solution)/shard_map/attend/pallas_call | solution.py:156
  55.9 1.3 %combine.1 = bf16[256,1024]{1,0:T(8,128)(2,1)} custom-call(bf16[96,256]{1,0:T(8,128)(2,1)S(1)} %get-tuple-element.28.outs_0_.high_ref, bf16[96,256]{1,0:T(8,128)(2,1)S(1)} %get-tuple-element.34.low_ref, bf16[24,1024]{1,0:T(8,128)(2,1)S(1)} %get-tuple-element.33.refs_0_, bf16[24,1024]{1,0:T(8,128)(2,1)S(1)} %collective-permute-done.13.refs_1_, ...), custom_call_target="tpu_custom_call" | custom-call | flops 100663296 | bytes 622592 | tf_op jit(solution)/shard_map/combine/pallas_call | solution.py:428
  (44 shorter events, 0.8 us)
Async XLA Ops:
  2.4 17.5 %copy-start.4 = (s32[256,8]{0,1:T(8,128)S(1)}, s32[256,8]{0,1:T(8,128)}, u32[]{:S(2)}) copy-start(s32[256,8]{0,1:T(8,128)} %param.23) | copy-start | bytes 24580
  2.4 17.5 %copy-start.6 = (bf16[128,4096]{1,0:T(8,128)(2,1)S(1)}, bf16[128,4096]{1,0:T(8,128)(2,1)}, u32[]{:S(2)}) copy-start(bf16[128,4096]{1,0:T(8,128)(2,1)} %refs_0_.5) | copy-start | bytes 3145732
  2.4 16.7 %collective-permute-start = (bf16[528,256]{1,0:T(8,128)(2,1)}, bf16[528,256]{1,0:T(8,128)(2,1)S(1)}, u32[]{:S(2)}, u32[]{:S(2)}) collective-permute-start(bf16[528,256]{1,0:T(8,128)(2,1)} %pack.1.refs_3_), channel_id=1, source_target_pairs={{0,8},{4,12},{8,0},{12,4},{1,9},{5,13},{9,1},{13,5},{2,10},{6,14},... | collective-permute-start | bytes 811016 | tf_op jit(solution)/shard_map/ppermute | solution.py:502
  6.5 13.3 %collective-permute-start.3 = (bf16[528,256]{1,0:T(8,128)(2,1)}, bf16[528,256]{1,0:T(8,128)(2,1)S(1)}, u32[]{:S(2)}, u32[]{:S(2)}) collective-permute-start(bf16[528,256]{1,0:T(8,128)(2,1)} %pack.1.refs_3_), channel_id=1, source_target_pairs={{0,4},{4,0},{8,12},{12,8},{1,5},{5,1},{9,13},{13,9},{2,6},{6,2},{1... | collective-permute-start | bytes 811016 | tf_op jit(solution)/shard_map/ppermute | solution.py:502
  8.1 16.9 %collective-permute-start.5 = (bf16[528,256]{1,0:T(8,128)(2,1)}, bf16[528,256]{1,0:T(8,128)(2,1)S(1)}, u32[]{:S(2)}, u32[]{:S(2)}) collective-permute-start(bf16[528,256]{1,0:T(8,128)(2,1)} %pack.1.refs_3_), channel_id=1, source_target_pairs={{0,1},{1,0},{2,3},{3,2},{4,5},{5,4},{6,7},{7,6},{8,9},{9,8},{10,11... | collective-permute-start | bytes 811016 | tf_op jit(solution)/shard_map/ppermute | solution.py:450
  8.1 11.7 %collective-permute-start.6 = (bf16[128,4096]{1,0:T(8,128)(2,1)}, bf16[128,4096]{1,0:T(8,128)(2,1)S(1)}, u32[]{:S(2)}, u32[]{:S(2)}) collective-permute-start(bf16[128,4096]{1,0:T(8,128)(2,1)} %refs_0_.5), channel_id=1, source_target_pairs={{0,1},{1,0},{2,3},{3,2},{4,5},{5,4},{6,7},{7,6},{8,9},{9,8},{10,11... | collective-permute-start | bytes 3145736 | tf_op jit(solution)/shard_map/ppermute | solution.py:450
  19.1 18.2 %collective-permute-start.1 = (bf16[528,256]{1,0:T(8,128)(2,1)S(1)}, bf16[528,256]{1,0:T(8,128)(2,1)S(1)}, u32[]{:S(2)}, u32[]{:S(2)}) collective-permute-start(bf16[528,256]{1,0:T(8,128)(2,1)S(1)} %collective-permute-done.refs_1_), channel_id=1, source_target_pairs={{0,4},{4,0},{8,12},{12,8},{1,5},{5,1},{9,13},{13,9},{2,6},{6,2},{1... | collective-permute-start | bytes 811016 | tf_op jit(solution)/shard_map/ppermute | solution.py:503
  19.8 11.3 %collective-permute-start.4 = (bf16[528,256]{1,0:T(8,128)(2,1)S(1)}, bf16[528,256]{1,0:T(8,128)(2,1)S(1)}, u32[]{:S(2)}, u32[]{:S(2)}) collective-permute-start(bf16[528,256]{1,0:T(8,128)(2,1)S(1)} %collective-permute-done.3.refs_1_), channel_id=1, source_target_pairs={{0,1},{1,0},{2,3},{3,2},{4,5},{5,4},{6,7},{7,6},{8,9},{9,8},{10,11... | collective-permute-start | bytes 811016 | tf_op jit(solution)/shard_map/ppermute | solution.py:450
  19.9 6.6 %copy-start.3 = (bf16[528,256]{1,0:T(8,128)(2,1)S(1)}, bf16[528,256]{1,0:T(8,128)(2,1)}, u32[]{:S(2)}) copy-start(bf16[528,256]{1,0:T(8,128)(2,1)} %pack.1.refs_3_) | copy-start | bytes 811012
  19.9 6.6 %copy-start.7 = (bf16[128,4096]{1,0:T(8,128)(2,1)S(1)}, bf16[128,4096]{1,0:T(8,128)(2,1)}, u32[]{:S(2)}) copy-start(bf16[128,4096]{1,0:T(8,128)(2,1)} %refs_0_.9) | copy-start | bytes 3145732
  19.9 6.5 %copy-start.8 = (bf16[128,512]{1,0:T(8,128)(2,1)S(1)}, bf16[128,512]{1,0:T(8,128)(2,1)}, u32[]{:S(2)}) copy-start(bf16[128,512]{1,0:T(8,128)(2,1)} %refs_1_.1) | copy-start | bytes 393220
  19.9 6.5 %copy-start.9 = (bf16[128,512]{1,0:T(8,128)(2,1)S(1)}, bf16[128,512]{1,0:T(8,128)(2,1)}, u32[]{:S(2)}) copy-start(bf16[128,512]{1,0:T(8,128)(2,1)} %refs_2_.1) | copy-start | bytes 393220
  21.5 13.5 %collective-permute-start.8 = (bf16[24,2048]{1,0:T(8,128)(2,1)S(1)}, bf16[24,2048]{1,0:T(8,128)(2,1)S(1)}, u32[]{:S(2)}, u32[]{:S(2)}) collective-permute-start(bf16[24,2048]{1,0:T(8,128)(2,1)S(1)} %get-tuple-element.25), channel_id=1, source_target_pairs={{0,4},{4,0},{8,12},{12,8},{1,5},{5,1},{9,13},{13,9},{2,6},{6,2},{1... | collective-permute-start | bytes 294920 | tf_op jit(solution)/shard_map/ppermute | solution.py:494
  22.9 12.2 %collective-permute-start.9 = (bf16[24,2048]{1,0:T(8,128)(2,1)S(1)}, bf16[24,2048]{1,0:T(8,128)(2,1)S(1)}, u32[]{:S(2)}, u32[]{:S(2)}) collective-permute-start(bf16[24,2048]{1,0:T(8,128)(2,1)S(1)} %get-tuple-element.26), channel_id=1, source_target_pairs={{0,8},{4,12},{8,0},{12,4},{1,9},{5,13},{9,1},{13,5},{2,10},{6,14},... | collective-permute-start | bytes 294920 | tf_op jit(solution)/shard_map/ppermute | solution.py:494
  25.0 10.6 %collective-permute-start.10 = (bf16[24,2048]{1,0:T(8,128)(2,1)S(1)}, bf16[24,2048]{1,0:T(8,128)(2,1)S(1)}, u32[]{:S(2)}, u32[]{:S(2)}) collective-permute-start(bf16[24,2048]{1,0:T(8,128)(2,1)S(1)} %get-tuple-element.27), channel_id=1, source_target_pairs={{0,12},{4,8},{8,4},{12,0},{1,13},{5,9},{9,5},{13,1},{2,14},{6,10},... | collective-permute-start | bytes 294920 | tf_op jit(solution)/shard_map/ppermute | solution.py:494
  31.1 4.4 %copy-start = (bf16[1,2048,768]{2,1,0:T(8,128)(2,1)S(1)}, bf16[1,2048,768]{2,1,0:T(8,128)(2,1)}, u32[]{:S(2)}) copy-start(bf16[1,2048,768]{2,1,0:T(8,128)(2,1)} %gate_ref.1) | copy-start | bytes 9437188
  31.1 4.4 %copy-start.1 = (bf16[1,2048,768]{2,1,0:T(8,128)(2,1)S(1)}, bf16[1,2048,768]{2,1,0:T(8,128)(2,1)}, u32[]{:S(2)}) copy-start(bf16[1,2048,768]{2,1,0:T(8,128)(2,1)} %up_ref.1) | copy-start | bytes 9437188
  36.7 1.6 %collective-permute-start.11 = (bf16[96,1536]{1,0:T(8,128)(2,1)S(1)}, bf16[96,1536]{1,0:T(8,128)(2,1)S(1)}, u32[]{:S(2)}, u32[]{:S(2)}) collective-permute-start(bf16[96,1536]{1,0:T(8,128)(2,1)S(1)} %gateup.1.refs_0_.mine_ref), channel_id=1, source_target_pairs={{0,1},{1,0},{2,3},{3,2},{4,5},{5,4},{6,7},{7,6},{8,9},{9,8},{10,11... | collective-permute-start | bytes 884744 | tf_op jit(solution)/shard_map/ppermute | solution.py:450
  36.8 3.8 %collective-permute-start.7 = (bf16[528,256]{1,0:T(8,128)(2,1)S(1)}, bf16[528,256]{1,0:T(8,128)(2,1)S(1)}, u32[]{:S(2)}, u32[]{:S(2)}) collective-permute-start(bf16[528,256]{1,0:T(8,128)(2,1)S(1)} %collective-permute-done.refs_1_), channel_id=1, source_target_pairs={{0,1},{1,0},{2,3},{3,2},{4,5},{5,4},{6,7},{7,6},{8,9},{9,8},{10,11... | collective-permute-start | bytes 811016 | tf_op jit(solution)/shard_map/ppermute | solution.py:450
  37.3 13.4 %collective-permute-start.2 = (bf16[528,256]{1,0:T(8,128)(2,1)S(1)}, bf16[528,256]{1,0:T(8,128)(2,1)S(1)}, u32[]{:S(2)}, u32[]{:S(2)}) collective-permute-start(bf16[528,256]{1,0:T(8,128)(2,1)S(1)} %collective-permute-done.1.refs_1_), channel_id=1, source_target_pairs={{0,1},{1,0},{2,3},{3,2},{4,5},{5,4},{6,7},{7,6},{8,9},{9,8},{10,11... | collective-permute-start | bytes 811016 | tf_op jit(solution)/shard_map/ppermute | solution.py:450
  39.0 7.1 %collective-permute-start.12 = (bf16[96,1024]{1,0:T(8,128)(2,1)S(1)}, bf16[96,1024]{1,0:T(8,128)(2,1)S(1)}, u32[]{:S(2)}, u32[]{:S(2)}) collective-permute-start(bf16[96,1024]{1,0:T(8,128)(2,1)S(1)} %get-tuple-element.32), channel_id=1, source_target_pairs={{0,2},{2,0},{1,3},{3,1},{4,6},{6,4},{5,7},{7,5},{8,10},{10,8},{9,1... | collective-permute-start | bytes 589832 | tf_op jit(solution)/shard_map/ppermute | solution.py:542
  46.2 9.7 %collective-permute-start.13 = (bf16[24,1024]{1,0:T(8,128)(2,1)S(1)}, bf16[24,1024]{1,0:T(8,128)(2,1)S(1)}, u32[]{:S(2)}, u32[]{:S(2)}) collective-permute-start(bf16[24,1024]{1,0:T(8,128)(2,1)S(1)} %get-tuple-element.35), channel_id=1, source_target_pairs={{4,0},{0,4},{12,8},{8,12},{5,1},{1,5},{13,9},{9,13},{6,2},{2,6},{1... | collective-permute-start | bytes 147464 | tf_op jit(solution)/shard_map/ppermute | solution.py:548
  46.4 9.5 %collective-permute-start.14 = (bf16[24,1024]{1,0:T(8,128)(2,1)S(1)}, bf16[24,1024]{1,0:T(8,128)(2,1)S(1)}, u32[]{:S(2)}, u32[]{:S(2)}) collective-permute-start(bf16[24,1024]{1,0:T(8,128)(2,1)S(1)} %get-tuple-element.36), channel_id=1, source_target_pairs={{8,0},{12,4},{0,8},{4,12},{9,1},{13,5},{1,9},{5,13},{10,2},{14,6},... | collective-permute-start | bytes 147464 | tf_op jit(solution)/shard_map/ppermute | solution.py:548
  48.8 7.1 %collective-permute-start.15 = (bf16[24,1024]{1,0:T(8,128)(2,1)S(1)}, bf16[24,1024]{1,0:T(8,128)(2,1)S(1)}, u32[]{:S(2)}, u32[]{:S(2)}) collective-permute-start(bf16[24,1024]{1,0:T(8,128)(2,1)S(1)} %get-tuple-element.37), channel_id=1, source_target_pairs={{12,0},{8,4},{4,8},{0,12},{13,1},{9,5},{5,9},{1,13},{14,2},{10,6},... | collective-permute-start | bytes 147464 | tf_op jit(solution)/shard_map/ppermute | solution.py:548
  (2 other events, 4.6 us)
